TPU v7x, 32 devices: a whole 2x2x4 slice. The times are simulated.
32 devices in a mesh: gx: 8 (over z, core), gy: 4 (over y, x).
Axes of the slice: x: 2, y: 2, z: 4, core: 2. Of those that a mesh axis runs over, the one named last changes fastest.
Arguments:
- suction_potential: float32 [64, 32, 128], P('gx', 'gy'), may hold values from -3 to 0.3
- ground_warmth: float32 [64, 32, 128], P('gx', 'gy'), may hold values from -4 to 4
- ground_category: int32 [64, 32, 128], P('gx', 'gy'), may hold values from 0 to 11
- icebound_flag: int32 [64, 32, 128], P('gx', 'gy'), may hold values 0 or 1
- ground_wetted_permeability: float32 [12], replicated, may hold values from 0.02 to 0.15
- ground_falloff_exponent: float32 [12], replicated, may hold values from 0.3 to 1.5
- camera_skew_per_plane: float32 [4], replicated, may hold values from -1 to 1
- hue_gradient_steepness: float32 [3], replicated, may hold values from 4 to 16
- hue_gradient_middles: float32 [3], replicated, may hold values from 0.1 to 0.4
- camera_distance_ordering: int32 [4, 4], replicated, may hold values from 0 to 3, as said below
Outputs:
- head_out: float32 [64, 32, 128], P('gx', 'gy')
- temp_out: float32 [64, 32, 128], P('gx', 'gy')
- image: float32 [4, 4, 64, 128], P(None, None, 'gx', 'gy')
Inputs may be any that keep to these rules, and one draw needn't show every extreme that they name: Each row of camera_distance_ordering names every slab 0 to 3 once.
All inputs are finite; a program needn't handle non-finite values. No bound on the sum of `icebound_flag` on one device may be relied on, other than what follows from the above.
Results may differ from a plain program's by a relative error of at most 0.0003.
Values sent between devices are 32-bit elements; how exact they have to be, the bound alone decides.
No kernel may reach another device: no remote copies, remote signals or barrier semaphores. Data moves between devices by JAX's collectives and lax.ppermute only.
A program may use at most 64 MiB of HBM per device.

v0:
```python
import jax
import jax.numpy as jnp
from jax import lax
from jax.sharding import PartitionSpec as P

STEPS = 2


IMPEDANCE = 4.0
DIFFUSE = 0.12


def with_halo(x, sides, width):
    for axis, dim in sides:
        count, length = (lax.axis_size(axis), x.shape[dim])
        up = [(i, (i + 1) % count) for i in range(count - 1)]
        down = [(j, i) for i, j in up]
        last = lax.slice_in_dim(x, length - width, length, axis=dim)
        first = lax.slice_in_dim(x, 0, width, axis=dim)
        before = lax.ppermute(last, axis, up)
        after = lax.ppermute(first, axis, down)
        x = jnp.concatenate([before, x, after], axis=dim)
    return x


def voxel_index_map(ground_category, table):
    total = jnp.zeros(ground_category.shape, jnp.float32)
    for number in range(table.shape[0]):
        total = total + jnp.where(ground_category == number, table[number], jnp.float32(0.0))
    return total


def advance(evolving_arrays, first_row, first_col, rows_all, cols_all):
    suction_potential, temp, conduct_sat, alpha, ice = evolving_arrays
    conduct = (
        conduct_sat
        * jnp.exp(alpha * jnp.minimum(suction_potential, 0.0))
        * jnp.exp(-IMPEDANCE * ice * jax.nn.sigmoid(-2.0 * temp))
    )
    global_rows = first_row + jnp.arange(suction_potential.shape[0], dtype=jnp.int32)
    global_cols = first_col + jnp.arange(suction_potential.shape[1], dtype=jnp.int32)
    open_rows = ((global_rows[:-1] >= 0) & (global_rows[1:] <= rows_all - 1))[:, None, None]
    open_cols = ((global_cols[:-1] >= 0) & (global_cols[1:] <= cols_all - 1))[None, :, None]
    flux_rows = jnp.where(
        open_rows,
        0.5 * (conduct[1:] + conduct[:-1]) * (suction_potential[1:] - suction_potential[:-1]),
        0.0,
    )
    flux_cols = jnp.where(
        open_cols,
        0.5
        * (conduct[:, 1:] + conduct[:, :-1])
        * (suction_potential[:, 1:] - suction_potential[:, :-1]),
        0.0,
    )
    flux_up = (
        0.5
        * (conduct[..., 1:] + conduct[..., :-1])
        * (suction_potential[..., 1:] - suction_potential[..., :-1] + 1.0)
    )
    zeros_up = jnp.zeros(suction_potential.shape[:2] + (1,), suction_potential.dtype)
    change_up = jnp.concatenate([flux_up, zeros_up], 2) - jnp.concatenate([zeros_up, flux_up], 2)
    change = (
        flux_rows[1:, 1:-1]
        - flux_rows[:-1, 1:-1]
        + (flux_cols[1:-1, 1:] - flux_cols[1:-1, :-1])
        + change_up[1:-1, 1:-1]
    )
    inside = ((global_rows[1:-1] >= 0) & (global_rows[1:-1] <= rows_all - 1))[:, None, None] & (
        (global_cols[1:-1] >= 0) & (global_cols[1:-1] <= cols_all - 1)
    )[None, :, None]
    head_new = jnp.where(inside, suction_potential[1:-1, 1:-1] + change, 0.0)
    vertical = jnp.concatenate([temp[..., 1:], zeros_up], 2) + jnp.concatenate(
        [zeros_up, temp[..., :-1]], 2
    )
    laplace = (
        temp[2:, 1:-1]
        + temp[:-2, 1:-1]
        + temp[1:-1, 2:]
        + temp[1:-1, :-2]
        + vertical[1:-1, 1:-1]
        - 6.0 * temp[1:-1, 1:-1]
    )
    temp_new = jnp.where(inside, temp[1:-1, 1:-1] + DIFFUSE * laplace, 0.0)
    return (head_new, temp_new, conduct_sat[1:-1, 1:-1], alpha[1:-1, 1:-1], ice[1:-1, 1:-1])


def moisture(suction_potential):
    return 0.05 + 0.4 * jnp.exp(0.8 * jnp.minimum(suction_potential, 0.0))


def render(theta, first_plane, planes_all, groups, tilt, gain, middle):
    depth_z = theta.shape[2]
    planes = first_plane + jnp.arange(theta.shape[1], dtype=jnp.int32)
    shift = tilt * (planes.astype(jnp.float32) - 0.5 * planes_all)
    wrapped = shift - depth_z * jnp.floor(shift / depth_z)
    base = jnp.floor(wrapped)
    frac = wrapped - base
    offset = base.astype(jnp.int32) % depth_z
    doubled = jnp.concatenate([theta, theta], 2)

    def plane_slices(column, start):
        lower_part = lax.dynamic_slice_in_dim(column, start, depth_z, 1)
        upper_part = lax.dynamic_slice_in_dim(column, start + 1, depth_z, 1)
        return (lower_part, upper_part)

    lower_vals, upper_vals = jax.vmap(plane_slices, in_axes=(1, 0), out_axes=(1, 1))(
        doubled, offset
    )
    sample = (1.0 - frac)[None, :, None] * lower_vals + frac[None, :, None] * upper_vals
    shape_four = (theta.shape[0], groups, theta.shape[1] // groups, depth_z)
    sample = sample.reshape(shape_four)
    optical = sample * (8.0 / planes_all)
    before = jnp.cumsum(optical, axis=2) - optical
    weight = (1.0 - jnp.exp(-optical)) * jnp.exp(-before)
    layers = [
        jnp.sum(jax.nn.sigmoid(gain[color] * (sample - middle[color])) * weight, axis=2)
        for color in range(3)
    ]
    layers.append(jnp.sum(optical, axis=2))
    return jnp.stack(layers, 0).transpose(2, 0, 1, 3)


def shards(
    suction_potential,
    ground_warmth,
    ground_category,
    icebound_flag,
    ground_wetted_permeability,
    ground_falloff_exponent,
    camera_skew_per_plane,
    hue_gradient_steepness,
    hue_gradient_middles,
    camera_distance_ordering,
):
    rows_dev = suction_potential.shape[0]
    cols_dev = suction_potential.shape[1]
    rows_all = rows_dev * lax.axis_size("gx")
    cols_all = cols_dev * lax.axis_size("gy")
    row_start = lax.axis_index("gx") * rows_dev
    col_start = lax.axis_index("gy") * cols_dev
    evolving_arrays = (
        suction_potential,
        ground_warmth,
        voxel_index_map(ground_category, ground_wetted_permeability),
        voxel_index_map(ground_category, ground_falloff_exponent),
        icebound_flag.astype(jnp.float32),
    )
    extended = with_halo(jnp.stack(evolving_arrays), (("gx", 1), ("gy", 2)), STEPS)
    evolving_arrays = tuple((extended[number] for number in range(5)))
    for number in range(STEPS):
        margin = STEPS - number
        evolving_arrays = advance(
            evolving_arrays, row_start - margin, col_start - margin, rows_all, cols_all
        )
    theta = moisture(evolving_arrays[0])

    def one_view(tilt):
        return render(
            theta, col_start, cols_all, 1, tilt, hue_gradient_steepness, hue_gradient_middles
        )[0]

    pieces = lax.map(one_view, camera_skew_per_plane)
    received = lax.all_to_all(pieces[None], "gy", split_axis=4, concat_axis=0, tiled=True)
    in_front = (camera_distance_ordering[:, None, :] < camera_distance_ordering[:, :, None]).astype(
        jnp.float32
    )
    depth = received[:, :, 3]
    front = jnp.einsum("vij,jvxz->ivxz", in_front, depth, precision=lax.Precision.HIGHEST)
    color = jnp.sum(jnp.exp(-front)[:, :, None] * received[:, :, :3], axis=0)
    opacity = 1.0 - jnp.exp(-jnp.sum(depth, axis=0))
    image = jnp.concatenate([color, opacity[:, None]], 1)
    return (evolving_arrays[0], evolving_arrays[1], image)


def solution(mesh):
    placed = (
        P("gx", "gy", None),
        P("gx", "gy", None),
        P("gx", "gy", None),
        P("gx", "gy", None),
        P(),
        P(),
        P(),
        P(),
        P(),
        P(),
    )
    return jax.shard_map(
        shards,
        mesh=mesh,
        in_specs=placed,
        out_specs=(P("gx", "gy", None), P("gx", "gy", None), P(None, None, "gx", "gy")),
        check_vma=False,
    )
```

profile of v0, /device:TPU:1, one launch (start us, length us, event | category | flops | bytes accessed | tf_op | source)
XLA Modules:
  0.0 95.6 jit_solution(1274984922315434157)
XLA Ops:
  0.6 1.8 %fusion.79 = (f32[1]{0:T(128)}, f32[1]{0:T(128)}, f32[1]{0:T(128)}, f32[1]{0:T(128)}, f32[1]{0:T(128)}, /*index=5*/f32[1]{0:T(128)}, f32[1]{0:T(128)}, f32[1]{0:...) fusion(f32[12]{0:T(128)} %param.16), kind=kLoop, calls=%fused_computation.171 | loop fusion | bytes 96 | tf_op jit(solution)/shard_map/slice | solution.py:29
  2.4 0.8 bitcast_dynamic-update-slice_fusion.4
  3.2 0.7 fusion.78
  3.9 0.7 copy-done.5
  4.7 7.6 %bitcast_dynamic-update-slice_fusion.2 = (f32[5,8,8,128]{3,2,1,0:T(8,128)S(1)}, pred[8,8,128]{2,1,0:T(8,128)(4,1)S(1)}, pred[8,8,128]{2,1,0:T(8,128)(4,1)S(1)}, ...) fusion(f32[5,8,8,128]{3,2,1,0:T(8,128)S(1)} %bitcast_dynamic-up, ...), kind=kLoop, calls=%fused_computation.130 | loop fusion | flops 286720 | bytes 163888
  12.3 7.6 %bitcast_dynamic-update-slice_fusion.1 = f32[5,8,8,128]{3,2,1,0:T(8,128)S(1)} fusion(f32[5,8,8,128]{3,2,1,0:T(8,128)S(1)} %get-tuple-element.160, pred[8,8,128]{2,1,0:T(8,128)(4,1)S(1)} %get-tuple-element.172, pred[8,8,128]{2,1,0:T(8,128)(4,1)S(1)} %get-tuple-element.171, pred[8,8,128]{2,1,0:T(8,128)(4,1)S(1)} %get-tuple-element.170, ...), kind=kLoop, calls=%fused_computation.129 | loop fusion | flops 188416 | bytes 131120
  19.9 4.6 %collective-permute-start = (f32[5,2,8,128]{3,2,1,0:T(8,128)S(1)}, f32[5,2,8,128]{3,2,1,0:T(8,128)S(1)}, u32[]{:S(2)}, u32[]{:S(2)}) collective-permute-start(f32[5,2,8,128]{3,2,1,0:T(8,128)S(1)} %get-tuple-element.191), channel_id=1, source_target_pairs={{0,4},{4,8},{8,12},{12,16},{16,20},{20,24},{24,28},{1,5},{5,9},{9,... | collective-permute-start | bytes 122888 | tf_op jit(solution)/shard_map/ppermute | solution.py:20
  24.5 1.9 %collective-permute-start.1 = (f32[5,2,8,128]{3,2,1,0:T(8,128)S(1)}, f32[5,2,8,128]{3,2,1,0:T(8,128)S(1)}, u32[]{:S(2)}, u32[]{:S(2)}) collective-permute-start(f32[5,2,8,128]{3,2,1,0:T(8,128)S(1)} %get-tuple-element.192), channel_id=1, source_target_pairs={{4,0},{8,4},{12,8},{16,12},{20,16},{24,20},{28,24},{5,1},{9,5},{13... | collective-permute-start | bytes 122888 | tf_op jit(solution)/shard_map/ppermute | solution.py:21
  27.0 2.8 %collective-permute-done.1 = f32[5,2,8,128]{3,2,1,0:T(8,128)S(1)} collective-permute-done((f32[5,2,8,128]{3,2,1,0:T(8,128)S(1)}, f32[5,2,8,128]{3,2,1,0:T(8,128)S(1)}, u32[]{:S(2)}, u32[]{:S(2)}) %collective-permute-start.1) | collective-permute-done | bytes 40992 | tf_op jit(solution)/shard_map/ppermute | solution.py:21
  29.9 3.1 %collective-permute-start.2 = (f32[5,12,2,128]{3,2,1,0:T(2,128)S(1)}, f32[5,12,2,128]{3,2,1,0:T(2,128)S(1)}, u32[]{:S(2)}, u32[]{:S(2)}) collective-permute-start(f32[5,12,2,128]{3,2,1,0:T(2,128)S(1)} %get-tuple-element.189), channel_id=1, source_target_pairs={{0,1},{1,2},{2,3},{4,5},{5,6},{6,7},{8,9},{9,10},{10,11},{12,13},{... | collective-permute-start | bytes 184328 | tf_op jit(solution)/shard_map/ppermute | solution.py:20
  33.0 1.3 %collective-permute-start.3 = (f32[5,12,2,128]{3,2,1,0:T(2,128)S(1)}, f32[5,12,2,128]{3,2,1,0:T(2,128)S(1)}, u32[]{:S(2)}, u32[]{:S(2)}) collective-permute-start(f32[5,12,2,128]{3,2,1,0:T(2,128)S(1)} %get-tuple-element.190), channel_id=1, source_target_pairs={{1,0},{2,1},{3,2},{5,4},{6,5},{7,6},{9,8},{10,9},{11,10},{13,12},{... | collective-permute-start | bytes 184328 | tf_op jit(solution)/shard_map/ppermute | solution.py:21
  34.4 3.6 %collective-permute-done.3 = f32[5,12,2,128]{3,2,1,0:T(2,128)S(1)} collective-permute-done((f32[5,12,2,128]{3,2,1,0:T(2,128)S(1)}, f32[5,12,2,128]{3,2,1,0:T(2,128)S(1)}, u32[]{:S(2)}, u32[]{:S(2)}) %collective-permute-start.3) | collective-permute-done | bytes 61472 | tf_op jit(solution)/shard_map/ppermute | solution.py:21
  39.1 0.7 multiply_add_fusion.1
  40.5 40.9 %while.12 = (s32[]{:T(128)}, f32[4,4,8,128]{3,2,1,0:T(8,128)S(1)}, f32[3]{0:T(128)S(1)}, f32[4]{0:T(128)S(1)}, s32[]{:T(128)}, /*index=5*/f32[8,8,256]{0,1,2:T(8,128)S(1)}, f32[3]{0:T(128)S(1)}, s32[]{:T(128)}) while((s32[]{:T(128)}, f32[4,4,8,128]{3,2,1,0:T(8,128)S(1)}, f32[3]{0:T(128)S(1)}, f32[4]{0:T(128)S(1)}, s32[]{:T(128)}, ...), condition=%wide.region_6.7_spmd, body=%wide.region_0.6_spmd.sunk | while | flops 352634 | bytes 442941 | solution.py:163
  40.5 0.6 dynamic_slice.8
  41.2 0.6 or_bitcast_fusion.2
  41.8 1.3 %gather_fusion = f32[8,8,128]{1,0,2:T(8,128)S(1)} fusion(f32[8,8,256]{1,0,2:T(8,128)S(1)} %bitcast.158, s32[8]{0:T(128)S(1)} %get-tuple-element.290), kind=kCustom, calls=%fused_computation.1.clone.1 | custom fusion | bytes 65632 | tf_op jit(solution)/shard_map/while/body/eval_jaxpr/vmap()/gather | solution.py:104
  43.3 1.3 %gather_fusion.1 = f32[8,8,128]{1,0,2:T(8,128)S(1)} fusion(f32[8,8,256]{1,0,2:T(8,128)S(1)} %bitcast.159, s32[8]{0:T(128)S(1)} %get-tuple-element.292), kind=kCustom, calls=%fused_computation.clone.1 | custom fusion | bytes 65632 | tf_op jit(solution)/shard_map/while/body/eval_jaxpr/vmap()/gather | solution.py:103
  44.9 0.7 fusion.83
  45.6 0.6 broadcast_subtract_fusion.2
  46.2 3.9 %fusion.84 = (f32[8,128]{1,0:T(8,128)S(1)}, f32[8,128]{1,0:T(8,128)S(1)}, f32[8,128]{1,0:T(8,128)S(1)}, f32[8,128]{1,0:T(8,128)S(1)}) fusion(f32[]{:T(128)} %bitcast.146, f32[]{:T(128)} %bitcast.147, f32[]{:T(128)} %bitcast.148, f32[]{:T(128)} %bitcast.149, f32[]{:T(128)} %bitcast.150, f32[]{:T(128)} %bitcast.151, f32[8,8,128]{2,1,0:T(8,128)S(1)} %copy.67, ...), kind=kOutput, calls=%fused_computation.16.clone.1 | output fusion | flops 339968 | bytes 82008 | tf_op jit(solution)/shard_map/while/body/eval_jaxpr/jit(cumsum)/reduce_window_sum | solution.py:114
  50.7 0.7 dynamic_slice.8
  51.4 0.6 or_bitcast_fusion.2
  52.1 1.3 %gather_fusion = f32[8,8,128]{1,0,2:T(8,128)S(1)} fusion(f32[8,8,256]{1,0,2:T(8,128)S(1)} %bitcast.158, s32[8]{0:T(128)S(1)} %get-tuple-element.290), kind=kCustom, calls=%fused_computation.1.clone.1 | custom fusion | bytes 65632 | tf_op jit(solution)/shard_map/while/body/eval_jaxpr/vmap()/gather | solution.py:104
  53.6 1.3 %gather_fusion.1 = f32[8,8,128]{1,0,2:T(8,128)S(1)} fusion(f32[8,8,256]{1,0,2:T(8,128)S(1)} %bitcast.159, s32[8]{0:T(128)S(1)} %get-tuple-element.292), kind=kCustom, calls=%fused_computation.clone.1 | custom fusion | bytes 65632 | tf_op jit(solution)/shard_map/while/body/eval_jaxpr/vmap()/gather | solution.py:103
  55.1 0.7 fusion.83
  55.8 0.6 broadcast_subtract_fusion.2
  56.4 3.9 %fusion.84 = (f32[8,128]{1,0:T(8,128)S(1)}, f32[8,128]{1,0:T(8,128)S(1)}, f32[8,128]{1,0:T(8,128)S(1)}, f32[8,128]{1,0:T(8,128)S(1)}) fusion(f32[]{:T(128)} %bitcast.146, f32[]{:T(128)} %bitcast.147, f32[]{:T(128)} %bitcast.148, f32[]{:T(128)} %bitcast.149, f32[]{:T(128)} %bitcast.150, f32[]{:T(128)} %bitcast.151, f32[8,8,128]{2,1,0:T(8,128)S(1)} %copy.67, ...), kind=kOutput, calls=%fused_computation.16.clone.1 | output fusion | flops 339968 | bytes 82008 | tf_op jit(solution)/shard_map/while/body/eval_jaxpr/jit(cumsum)/reduce_window_sum | solution.py:114
  61.0 0.7 dynamic_slice.8
  61.6 0.6 or_bitcast_fusion.2
  62.3 1.3 %gather_fusion = f32[8,8,128]{1,0,2:T(8,128)S(1)} fusion(f32[8,8,256]{1,0,2:T(8,128)S(1)} %bitcast.158, s32[8]{0:T(128)S(1)} %get-tuple-element.290), kind=kCustom, calls=%fused_computation.1.clone.1 | custom fusion | bytes 65632 | tf_op jit(solution)/shard_map/while/body/eval_jaxpr/vmap()/gather | solution.py:104
  63.8 1.3 %gather_fusion.1 = f32[8,8,128]{1,0,2:T(8,128)S(1)} fusion(f32[8,8,256]{1,0,2:T(8,128)S(1)} %bitcast.159, s32[8]{0:T(128)S(1)} %get-tuple-element.292), kind=kCustom, calls=%fused_computation.clone.1 | custom fusion | bytes 65632 | tf_op jit(solution)/shard_map/while/body/eval_jaxpr/vmap()/gather | solution.py:103
  65.3 0.7 fusion.83
  66.0 0.6 broadcast_subtract_fusion.2
  66.7 3.9 %fusion.84 = (f32[8,128]{1,0:T(8,128)S(1)}, f32[8,128]{1,0:T(8,128)S(1)}, f32[8,128]{1,0:T(8,128)S(1)}, f32[8,128]{1,0:T(8,128)S(1)}) fusion(f32[]{:T(128)} %bitcast.146, f32[]{:T(128)} %bitcast.147, f32[]{:T(128)} %bitcast.148, f32[]{:T(128)} %bitcast.149, f32[]{:T(128)} %bitcast.150, f32[]{:T(128)} %bitcast.151, f32[8,8,128]{2,1,0:T(8,128)S(1)} %copy.67, ...), kind=kOutput, calls=%fused_computation.16.clone.1 | output fusion | flops 339968 | bytes 82008 | tf_op jit(solution)/shard_map/while/body/eval_jaxpr/jit(cumsum)/reduce_window_sum | solution.py:114
  71.2 0.7 dynamic_slice.8
  71.9 0.6 or_bitcast_fusion.2
  72.5 1.3 %gather_fusion = f32[8,8,128]{1,0,2:T(8,128)S(1)} fusion(f32[8,8,256]{1,0,2:T(8,128)S(1)} %bitcast.158, s32[8]{0:T(128)S(1)} %get-tuple-element.290), kind=kCustom, calls=%fused_computation.1.clone.1 | custom fusion | bytes 65632 | tf_op jit(solution)/shard_map/while/body/eval_jaxpr/vmap()/gather | solution.py:104
  74.0 1.3 %gather_fusion.1 = f32[8,8,128]{1,0,2:T(8,128)S(1)} fusion(f32[8,8,256]{1,0,2:T(8,128)S(1)} %bitcast.159, s32[8]{0:T(128)S(1)} %get-tuple-element.292), kind=kCustom, calls=%fused_computation.clone.1 | custom fusion | bytes 65632 | tf_op jit(solution)/shard_map/while/body/eval_jaxpr/vmap()/gather | solution.py:103
  75.6 0.7 fusion.83
  76.2 0.6 broadcast_subtract_fusion.2
  76.9 3.9 %fusion.84 = (f32[8,128]{1,0:T(8,128)S(1)}, f32[8,128]{1,0:T(8,128)S(1)}, f32[8,128]{1,0:T(8,128)S(1)}, f32[8,128]{1,0:T(8,128)S(1)}) fusion(f32[]{:T(128)} %bitcast.146, f32[]{:T(128)} %bitcast.147, f32[]{:T(128)} %bitcast.148, f32[]{:T(128)} %bitcast.149, f32[]{:T(128)} %bitcast.150, f32[]{:T(128)} %bitcast.151, f32[8,8,128]{2,1,0:T(8,128)S(1)} %copy.67, ...), kind=kOutput, calls=%fused_computation.16.clone.1 | output fusion | flops 339968 | bytes 82008 | tf_op jit(solution)/shard_map/while/body/eval_jaxpr/jit(cumsum)/reduce_window_sum | solution.py:114
  82.1 1.1 %reshape.252 = f32[4,1,4096]{2,1,0:T(1,128)S(1)} reshape(f32[128,1,4,4,8]{4,3,2,1,0:T(4,128)S(1)} %bitcast_bitcast_fusion) | data formatting | bytes 131072
  83.3 7.3 %all_to_all.18 = f32[4,1,4096]{2,1,0:T(1,128)S(1)} all-to-all(f32[4,1,4096]{2,1,0:T(1,128)S(1)} %reshape.252), channel_id=1, replica_groups=mesh['gx'=8,'gy'=4] {'gy'}, dimensions={0} | all-to-all | bytes 131072 | tf_op jit(solution)/shard_map/all_to_all | solution.py:164
  91.1 0.8 reduce.21
  91.9 1.3 %reshape.253 = f32[128,1,4,4,8]{4,3,2,1,0:T(4,128)S(1)} reshape(f32[4,4096]{1,0:T(4,128)S(1)} %reduce.21) | data formatting | bytes 131072
  93.8 0.6 copy-done.6
  94.9 0.6 copy.50
  (99 shorter events, 8.8 us)
Async XLA Ops:
  2.4 0.8 copy-start.2
  2.4 1.5 %copy-start.3 = (f32[8,8,128]{2,1,0:T(8,128)S(1)}, f32[8,8,128]{2,1,0:T(8,128)}, u32[]{:S(2)}) copy-start(f32[8,8,128]{2,1,0:T(8,128)} %param.13) | copy-start | bytes 98308
  3.9 0.8 copy-start.5
  12.3 7.6 %copy-start.4 = (s32[8,8,128]{2,1,0:T(8,128)S(1)}, s32[8,8,128]{2,1,0:T(8,128)}, u32[]{:S(2)}) copy-start(s32[8,8,128]{2,1,0:T(8,128)} %param.15) | copy-start | bytes 98308
  19.9 7.1 %collective-permute-start = (f32[5,2,8,128]{3,2,1,0:T(8,128)S(1)}, f32[5,2,8,128]{3,2,1,0:T(8,128)S(1)}, u32[]{:S(2)}, u32[]{:S(2)}) collective-permute-start(f32[5,2,8,128]{3,2,1,0:T(8,128)S(1)} %get-tuple-element.191), channel_id=1, source_target_pairs={{0,4},{4,8},{8,12},{12,16},{16,20},{20,24},{24,28},{1,5},{5,9},{9,... | collective-permute-start | bytes 122888 | tf_op jit(solution)/shard_map/ppermute | solution.py:20
  24.5 5.3 %collective-permute-start.1 = (f32[5,2,8,128]{3,2,1,0:T(8,128)S(1)}, f32[5,2,8,128]{3,2,1,0:T(8,128)S(1)}, u32[]{:S(2)}, u32[]{:S(2)}) collective-permute-start(f32[5,2,8,128]{3,2,1,0:T(8,128)S(1)} %get-tuple-element.192), channel_id=1, source_target_pairs={{4,0},{8,4},{12,8},{16,12},{20,16},{24,20},{28,24},{5,1},{9,5},{13... | collective-permute-start | bytes 122888 | tf_op jit(solution)/shard_map/ppermute | solution.py:21
  29.9 4.5 %collective-permute-start.2 = (f32[5,12,2,128]{3,2,1,0:T(2,128)S(1)}, f32[5,12,2,128]{3,2,1,0:T(2,128)S(1)}, u32[]{:S(2)}, u32[]{:S(2)}) collective-permute-start(f32[5,12,2,128]{3,2,1,0:T(2,128)S(1)} %get-tuple-element.189), channel_id=1, source_target_pairs={{0,1},{1,2},{2,3},{4,5},{5,6},{6,7},{8,9},{9,10},{10,11},{12,13},{... | collective-permute-start | bytes 184328 | tf_op jit(solution)/shard_map/ppermute | solution.py:20
  33.0 5.0 %collective-permute-start.3 = (f32[5,12,2,128]{3,2,1,0:T(2,128)S(1)}, f32[5,12,2,128]{3,2,1,0:T(2,128)S(1)}, u32[]{:S(2)}, u32[]{:S(2)}) collective-permute-start(f32[5,12,2,128]{3,2,1,0:T(2,128)S(1)} %get-tuple-element.190), channel_id=1, source_target_pairs={{1,0},{2,1},{3,2},{5,4},{6,5},{7,6},{9,8},{10,9},{11,10},{13,12},{... | collective-permute-start | bytes 184328 | tf_op jit(solution)/shard_map/ppermute | solution.py:21
  39.9 0.7 copy-start
  39.9 0.7 copy-start.1
  39.9 0.7 copy-start.7
  93.8 0.7 copy-start.6
where the time goes:
time: 96.9 us; the launch traced here: 95.6 us
  other arithmetic  39.2 us (40%)
  local copies, waits for them, and re-layouts  30.4 us (31%)
  starting transfers between devices  10.9 us (11%)
  blocking collectives  7.29 us (8%)
  waiting for transfers between devices  6.41 us (7%)
    another operation x4, other arithmetic, render(): before = jnp.cumsum(optical, axis=2) - optical  15.5 us
    unnamed x2, other arithmetic  15.2 us
    ppermute x2, starting transfers between devices, with_halo(): before = lax.ppermute(last, axis, up)  7.7 us
    all_to_all x1, blocking collectives, shards(): lax.all_to_all(pieces[None], 'gy', split_axis=4, concat_axis=0, tiled=True)  7.29 us
    ppermute x2, waiting for transfers between devices, with_halo(): after = lax.ppermute(first, axis, down)  6.41 us
    gather x8, local copies, waits for them, and re-layouts, plane_slices(): lower_part = lax.dynamic_slice_in_dim(column, start, depth_z, 1)  6.08 us
    gather x8, local copies, waits for them, and re-layouts, plane_slices(): upper_part = lax.dynamic_slice_in_dim(column, start + 1, depth_z, 1)  6 us
    unnamed x22, local copies, waits for them, and re-layouts  5.52 us
  transfers between devices with their start and end apart: 4, of which 2 were waited for; matrix products, arithmetic and copies ran while one was open for 1% of the time, Pallas kernels for 0%

commit v1 on v0

v1 whole, which is shorter than its diff:
```python
import functools

import jax
import jax.numpy as jnp
from jax import lax
from jax.experimental import pallas as pl
from jax.experimental.pallas import tpu as pltpu
from jax.sharding import PartitionSpec as P

STEPS = 2
IMPEDANCE = 4.0
DIFFUSE = 0.12

VMEM = pl.BlockSpec(memory_space=pltpu.VMEM)
SMEM = pl.BlockSpec(memory_space=pltpu.SMEM)


def pack_kernel(head_ref, temp_ref, soil_ref, ice_ref, out_ref):
    out_ref[0] = head_ref[...]
    out_ref[1] = temp_ref[...]
    out_ref[2] = soil_ref[...].astype(jnp.float32)
    out_ref[3] = ice_ref[...].astype(jnp.float32)


def column_of(peer, count, cols):
    at = lax.rem(lax.axis_index("gy") - peer + count, count)
    return pl.multiple_of(at * cols, cols)


def edge_kernel(count, *refs):
    blocks, (inner_ref, outer_ref) = refs[:count], refs[count:]
    rows, cols = blocks[0].shape[1:3]
    odd = lax.rem(lax.axis_index("gx"), 2)
    inner = (1 - odd) * (rows - STEPS)
    outer = odd * (rows - STEPS)
    for peer, block in enumerate(blocks):
        at = pl.ds(column_of(peer, count, cols), cols)
        inner_ref[:, :, at, :] = block[:, pl.ds(inner, STEPS)]
        outer_ref[:, :, at, :] = block[:, pl.ds(outer, STEPS)]


def conductivity(head, temp, ks, alpha, ice):
    frozen = (0.5 * IMPEDANCE) * ice * (1.0 - jnp.tanh(temp))
    return 0.5 * ks * jnp.exp(alpha * jnp.minimum(head, 0.0) - frozen)


def table_row(table_ref, lane):
    row = jnp.zeros(lane.shape, jnp.float32)
    for number in range(table_ref.shape[0]):
        row = jnp.where(lane == number, table_ref[number], row)
    return row


def scalar_floor(x):
    whole = x.astype(jnp.int32)
    return whole - (whole.astype(jnp.float32) > x).astype(jnp.int32)


def main_kernel(
    count,
    rows_count,
    ks_ref,
    alpha_ref,
    tilt_ref,
    gain_ref,
    middle_ref,
    rank_ref,
    *refs,
):
    blocks = refs[:count]
    inner_ref, outer_ref, head_ref, temp_ref, image_ref, all_ref, theta_ref = refs[count:]
    rows, cols, depth = blocks[0].shape[1:]
    width = count * cols
    strip = depth // count
    views = tilt_ref.shape[0]
    gx = lax.axis_index("gx")
    gy = lax.axis_index("gy")
    odd = lax.rem(gx, 2)

    for peer, block in enumerate(blocks):
        at = pl.ds(column_of(peer, count, cols), cols)
        all_ref[:, STEPS : STEPS + rows, at, :] = block[...]
    all_ref[:, pl.ds((1 - odd) * (rows + STEPS), STEPS)] = inner_ref[...]
    all_ref[:, pl.ds(odd * (rows + STEPS), STEPS)] = outer_ref[...]

    low = (gx > 0).astype(jnp.float32)
    high = (gx < rows_count - 1).astype(jnp.float32)
    shape = (width, depth)
    lane = lax.broadcasted_iota(jnp.int32, shape, 1)
    col = lax.broadcasted_iota(jnp.int32, shape, 0)
    up_open = lane < depth - 1
    down_open = lane > 0
    next_open = col < width - 1
    last_open = col > 0
    ks_row = table_row(ks_ref, lane)
    alpha_row = table_row(alpha_ref, lane)

    def look_up(table, index):
        return jnp.take_along_axis(table, index, axis=1, mode="promise_in_bounds")

    total = rows + 2 * STEPS
    head = [all_ref[0, r] for r in range(total)]
    temp = [all_ref[1, r] for r in range(total)]
    ice = [all_ref[3, r] for r in range(total)]
    soil = [all_ref[2, r].astype(jnp.int32) for r in range(total)]
    ks = [look_up(ks_row, s) for s in soil]
    alpha = [look_up(alpha_row, s) for s in soil]
    for step in range(STEPS):
        edge = STEPS - step
        k = [conductivity(*v) for v in zip(head, temp, ks, alpha, ice)]
        size = len(head)
        across = []
        for r in range(size - 1):
            flux = (k[r] + k[r + 1]) * (head[r + 1] - head[r])
            if r == edge - 1:
                flux = flux * low
            if r == size - edge - 1:
                flux = flux * high
            across.append(flux)
        temp[edge - 1] = temp[edge - 1] * low
        temp[size - edge] = temp[size - edge] * high
        new_head, new_temp = [], []
        for r in range(1, size - 1):
            h, t, c = head[r], temp[r], k[r]
            change = across[r] - across[r - 1]
            flux = (c + pltpu.roll(c, width - 1, 0)) * (pltpu.roll(h, width - 1, 0) - h)
            flux = jnp.where(next_open, flux, 0.0)
            change = change + (flux - pltpu.roll(flux, 1, 0))
            flux = (c + pltpu.roll(c, depth - 1, 1)) * (pltpu.roll(h, depth - 1, 1) - h + 1.0)
            flux = jnp.where(up_open, flux, 0.0)
            change = change + (flux - pltpu.roll(flux, 1, 1))
            new_head.append(h + change)
            near = temp[r - 1] + temp[r + 1]
            near = near + jnp.where(next_open, pltpu.roll(t, width - 1, 0), 0.0)
            near = near + jnp.where(last_open, pltpu.roll(t, 1, 0), 0.0)
            near = near + jnp.where(up_open, pltpu.roll(t, depth - 1, 1), 0.0)
            near = near + jnp.where(down_open, pltpu.roll(t, 1, 1), 0.0)
            new_temp.append(t + DIFFUSE * (near - 6.0 * t))
        head, temp = new_head, new_temp
        ks, alpha, ice = ks[1:-1], alpha[1:-1], ice[1:-1]

    for r in range(rows):
        theta = 0.05 + 0.4 * jnp.exp(0.8 * jnp.minimum(head[r], 0.0))
        theta_ref[r * width : (r + 1) * width] = theta
        all_ref[0, r] = head[r]
        all_ref[1, r] = temp[r]
    own = pl.ds(pl.multiple_of(gy * cols, cols), cols)
    head_ref[...] = all_ref[0, :rows, own, :]
    temp_ref[...] = all_ref[1, :rows, own, :]

    lane = lax.broadcasted_iota(jnp.int32, (rows, depth), 1)
    slab_of = lane // strip
    begin = gy * strip
    clear = [jnp.ones((rows, depth), jnp.float32) for _ in range(views)]
    thick = [jnp.zeros((rows, depth), jnp.float32) for _ in range(views)]
    shade = [[jnp.zeros((rows, depth), jnp.float32)] * 3 for _ in range(views)]
    for plane in range(cols):
        layers = []
        for slab in range(count):
            y = slab * cols + plane
            value = theta_ref[pl.ds(y, rows, stride=width), :]
            layers.append((value, pltpu.roll(value, depth - 1, 1) - value))
        for view in range(views):
            sample = None
            for slab in range(count):
                y = slab * cols + plane
                shift = tilt_ref[view] * jnp.float32(y - 0.5 * width)
                turns = scalar_floor(shift * (1.0 / depth))
                wrapped = shift - depth * turns.astype(jnp.float32)
                base = scalar_floor(wrapped)
                frac = wrapped - base.astype(jnp.float32)
                value, rise = layers[slab]
                move = (slab * strip - begin - base) & (depth - 1)
                moved = pltpu.roll(value + frac * rise, move, 1)
                sample = moved if slab == 0 else jnp.where(slab_of == slab, moved, sample)
            tau = sample * (8.0 / width)
            thick[view] = thick[view] + tau
            rest = clear[view] * jnp.exp(-tau)
            weight = 0.5 * (clear[view] - rest)
            clear[view] = rest
            for c in range(3):
                glow = jnp.tanh((0.5 * gain_ref[c]) * (sample - middle_ref[c]))
                shade[view][c] = shade[view][c] + (weight + weight * glow)

    def over_slabs(x):
        size = strip
        while size < depth:
            x = x + pltpu.roll(x, size, 1)
            size *= 2
        return x

    for view in range(views):
        rank = jnp.zeros((rows, depth), jnp.int32)
        for slab in range(count):
            rank = jnp.where(slab_of == slab, rank_ref[view, slab], rank)
        front = jnp.zeros((rows, depth), jnp.float32)
        for d in range(1, count):
            nearer = pltpu.roll(rank, d * strip, 1) < rank
            front = front + jnp.where(nearer, pltpu.roll(thick[view], d * strip, 1), 0.0)
        through = jnp.exp(-front)
        for c in range(3):
            image_ref[view, c] = over_slabs(through * shade[view][c])[:, :strip]
        image_ref[view, 3] = (1.0 - jnp.exp(-over_slabs(thick[view])))[:, :strip]


def shards(head, warmth, soil, icebound, ks, alpha, tilt, gain, middle, ranks):
    rows, cols, depth = head.shape
    count = lax.axis_size("gy")
    rows_count = lax.axis_size("gx")
    width = count * cols
    views = tilt.shape[0]
    assert depth & (depth - 1) == 0 and depth % count == 0
    assert count & (count - 1) == 0 and ranks.shape[1] == count

    packed = pl.pallas_call(
        pack_kernel,
        out_shape=jax.ShapeDtypeStruct((4, rows, cols, depth), jnp.float32),
        in_specs=[VMEM] * 4,
        out_specs=VMEM,
        name="pack",
    )(head, warmth, soil, icebound)
    blocks = [packed]
    for peer in range(1, count):
        ring = [(i, (i + peer) % count) for i in range(count)]
        blocks.append(lax.ppermute(packed, "gy", ring))

    border = jax.ShapeDtypeStruct((4, STEPS, width, depth), jnp.float32)
    inner, outer = pl.pallas_call(
        functools.partial(edge_kernel, count),
        out_shape=(border, border),
        in_specs=[VMEM] * count,
        out_specs=(VMEM, VMEM),
        name="edges",
    )(*blocks)
    pairs = [(i, i + 1) for i in range(rows_count - 1)]
    pairs = [pairs[0::2], pairs[1::2]]
    pairs = [p + [(b, a) for a, b in p] for p in pairs]
    outer = lax.ppermute(outer, "gx", pairs[1])
    inner = lax.ppermute(inner, "gx", pairs[0])

    cell = jax.ShapeDtypeStruct((rows, cols, depth), jnp.float32)
    return pl.pallas_call(
        functools.partial(main_kernel, count, rows_count),
        out_shape=(
            cell,
            cell,
            jax.ShapeDtypeStruct((views, 4, rows, depth // count), jnp.float32),
        ),
        in_specs=[SMEM] * 6 + [VMEM] * (count + 2),
        out_specs=(VMEM, VMEM, VMEM),
        scratch_shapes=[
            pltpu.VMEM((4, rows + 2 * STEPS, width, depth), jnp.float32),
            pltpu.VMEM((rows * width, depth), jnp.float32),
        ],
        name="steps_and_views",
    )(ks, alpha, tilt, gain, middle, ranks, *blocks, inner, outer)


def solution(mesh):
    cells = P("gx", "gy", None)
    return jax.shard_map(
        shards,
        mesh=mesh,
        in_specs=(cells,) * 4 + (P(),) * 6,
        out_specs=(cells, cells, P(None, None, "gx", "gy")),
        check_vma=False,
    )
```

time: 96.9 us -> 29.4 us (0.30); the launches traced: 95.6 us -> 29.2 us
  other arithmetic: 39.2 us -> 0 us
  local copies, waits for them, and re-layouts: 30.4 us -> 1.33 us
  Pallas kernels: 0 us -> 8.19 us
  blocking collectives: 7.29 us -> 0 us
  waiting for transfers between devices: 6.41 us -> 8.98 us
    another operation x5 -> x0, other arithmetic: 15.5 us -> none  [the longest x4 15.5 us: render(): before = jnp.cumsum(optical, axis=2) - optical]
    unnamed x2 -> x0, other arithmetic: 15.2 us -> none
    gather x16 -> x0, local copies, waits for them, and re-layouts: 12.1 us -> none  [the longest x8 6.08 us: plane_slices(): lower_part = lax.dynamic_slice_in_dim(column, start, depth_z, 1)]
    pallas_call x0 -> x3, Pallas kernels: none -> 8.19 us  [the longest x1 4.92 us: shards(): pl.pallas_call(functools.partial(main_kernel, count, rows_count), out_sha...]
    all_to_all x1 -> x0, blocking collectives: 7.29 us -> none  [shards(): lax.all_to_all(pieces[None], 'gy', split_axis=4, concat_axis=0, tiled=True)]
    slice x8 -> x0, local copies, waits for them, and re-layouts: 5.33 us -> none  [the longest x4 2.75 us: render(): gain[color] * (sample - middle[color])]
    unnamed x22 -> x10, local copies, waits for them, and re-layouts: 5.52 us -> 1.33 us
    while x18 -> x0, local copies, waits for them, and re-layouts: 2.79 us -> none
  transfers between devices with their start and end apart: 4 -> 5, of which waited for: 2 -> 4; matrix products, arithmetic and copies ran while one was open for 1% -> 0% of each run, Pallas kernels for 0% -> 0%
where the time goes in v1:
time: 29.4 us; the launch traced here: 29.2 us
  starting transfers between devices  10 us (34%)
  waiting for transfers between devices  8.98 us (31%)
  Pallas kernels  8.19 us (28%)
  local copies, waits for them, and re-layouts  1.33 us (5%)
  between operations  0.66 us (2%)
    ppermute x3, waiting for transfers between devices, shards(): blocks.append(lax.ppermute(packed, 'gy', ring))  5.6 us
    pallas_call x1, Pallas kernels, shards(): pl.pallas_call(functools.partial(main_kernel, count, rows_count), out_sha...  4.92 us
    ppermute x3, starting transfers between devices, shards(): blocks.append(lax.ppermute(packed, 'gy', ring))  3.52 us
    ppermute x1, starting transfers between devices, shards(): inner = lax.ppermute(inner, 'gx', pairs[0])  3.43 us
    ppermute x1, waiting for transfers between devices, shards(): outer = lax.ppermute(outer, 'gx', pairs[1])  3.38 us
    ppermute x1, starting transfers between devices, shards(): outer = lax.ppermute(outer, 'gx', pairs[1])  3.08 us
    pallas_call x1, Pallas kernels, shards(): pl.pallas_call(functools.partial(edge_kernel, count), out_shape=(border,...  1.81 us
    pallas_call x1, Pallas kernels, shards(): pl.pallas_call(pack_kernel, out_shape=jax.ShapeDtypeStruct((4, rows, cols...  1.46 us
  transfers between devices with their start and end apart: 5, of which 4 were waited for; matrix products, arithmetic and copies ran while one was open for 0% of the time, Pallas kernels for 0%

profile of v1, /device:TPU:1, one launch (start us, length us, event | category | flops | bytes accessed | tf_op | source)
XLA Modules:
  0.0 29.2 jit_solution(18158968081173718272)
XLA Ops:
  0.6 1.5 %pack.1.refs_0_ = f32[4,8,8,128]{3,2,1,0:T(8,128)} custom-call(f32[8,8,128]{2,1,0:T(8,128)} %head_ref.1, f32[8,8,128]{2,1,0:T(8,128)} %temp_ref.1, s32[8,8,128]{2,1,0:T(8,128)} %soil_ref.1, s32[8,8,128]{2,1,0:T(8,128)} %ice_ref.1), custom_call_target="tpu_custom_call" | custom-call | tf_op jit(solution)/shard_map/pack/pallas_call | solution.py:215
  2.1 3.0 %collective-permute-start.2 = (f32[4,8,8,128]{3,2,1,0:T(8,128)}, f32[4,8,8,128]{3,2,1,0:T(8,128)S(1)}, u32[]{:S(2)}, u32[]{:S(2)}) collective-permute-start(f32[4,8,8,128]{3,2,1,0:T(8,128)} %pack.1.refs_0_), channel_id=1, source_target_pairs={{0,3},{1,0},{2,1},{3,2},{4,7},{5,4},{6,5},{7,6},{8,11},{9,8},{10,9... | collective-permute-start | bytes 393224 | tf_op jit(solution)/shard_map/ppermute | solution.py:225
  5.1 0.2 collective-permute-start.1
  5.3 0.3 %collective-permute-start = (f32[4,8,8,128]{3,2,1,0:T(8,128)}, f32[4,8,8,128]{3,2,1,0:T(8,128)S(1)}, u32[]{:S(2)}, u32[]{:S(2)}) collective-permute-start(f32[4,8,8,128]{3,2,1,0:T(8,128)} %pack.1.refs_0_), channel_id=1, source_target_pairs={{0,1},{1,2},{2,3},{3,0},{4,5},{5,6},{6,7},{7,4},{8,9},{9,10},{10,1... | collective-permute-start | bytes 393224 | tf_op jit(solution)/shard_map/ppermute | solution.py:225
  5.6 2.0 %collective-permute-done.2.refs_3_ = f32[4,8,8,128]{3,2,1,0:T(8,128)S(1)} collective-permute-done((f32[4,8,8,128]{3,2,1,0:T(8,128)}, f32[4,8,8,128]{3,2,1,0:T(8,128)S(1)}, u32[]{:S(2)}, u32[]{:S(2)}) %collective-permute-start.2) | collective-permute-done | bytes 131104 | tf_op jit(solution)/shard_map/ppermute | solution.py:225
  7.7 0.0 copy-start
  7.7 2.3 %collective-permute-done.1.refs_2_ = f32[4,8,8,128]{3,2,1,0:T(8,128)S(1)} collective-permute-done((f32[4,8,8,128]{3,2,1,0:T(8,128)}, f32[4,8,8,128]{3,2,1,0:T(8,128)S(1)}, u32[]{:S(2)}, u32[]{:S(2)}) %collective-permute-start.1) | collective-permute-done | bytes 131104 | tf_op jit(solution)/shard_map/ppermute | solution.py:225
  9.9 0.0 copy-start.1
  9.9 1.3 %collective-permute-done.refs_1_ = f32[4,8,8,128]{3,2,1,0:T(8,128)S(1)} collective-permute-done((f32[4,8,8,128]{3,2,1,0:T(8,128)}, f32[4,8,8,128]{3,2,1,0:T(8,128)S(1)}, u32[]{:S(2)}, u32[]{:S(2)}) %collective-permute-start) | collective-permute-done | bytes 131104 | tf_op jit(solution)/shard_map/ppermute | solution.py:225
  11.2 0.0 copy-done
  11.2 0.0 copy-done.1
  11.2 0.0 copy-start.2
  11.2 0.7 %copy-done.2 = f32[4,8,8,128]{3,2,1,0:T(8,128)} copy-done((f32[4,8,8,128]{3,2,1,0:T(8,128)}, f32[4,8,8,128]{3,2,1,0:T(8,128)S(1)}, u32[]{:S(2)}) %copy-start.2) | copy-done | bytes 131096
  11.9 1.8 %edges.1 = (f32[4,2,32,128]{3,2,1,0:T(8,128)}, f32[4,2,32,128]{3,2,1,0:T(8,128)}) custom-call(f32[4,8,8,128]{3,2,1,0:T(8,128)} %pack.1.refs_0_, f32[4,8,8,128]{3,2,1,0:T(8,128)} %copy-done.2, f32[4,8,8,128]{3,2,1,0:T(8,128)} %copy-done.1, f32[4,8,8,128]{3,2,1,0:T(8,128)} %copy-done), custom_call_target="tpu_custom_call" | custom-call | tf_op jit(solution)/shard_map/edges/pallas_call | solution.py:228
  13.7 3.4 %collective-permute-start.3 = (f32[4,2,32,128]{3,2,1,0:T(8,128)}, f32[4,2,32,128]{3,2,1,0:T(8,128)S(1)}, u32[]{:S(2)}, u32[]{:S(2)}) collective-permute-start(f32[4,2,32,128]{3,2,1,0:T(8,128)} %get-tuple-element.5), channel_id=1, source_target_pairs={{0,4},{8,12},{16,20},{24,28},{4,0},{12,8},{20,16},{28,24},{1,5},{9... | collective-permute-start | bytes 393224 | tf_op jit(solution)/shard_map/ppermute | solution.py:239
  17.1 3.1 %collective-permute-start.4 = (f32[4,2,32,128]{3,2,1,0:T(8,128)}, f32[4,2,32,128]{3,2,1,0:T(8,128)S(1)}, u32[]{:S(2)}, u32[]{:S(2)}) collective-permute-start(f32[4,2,32,128]{3,2,1,0:T(8,128)} %get-tuple-element.6), channel_id=1, source_target_pairs={{4,8},{12,16},{20,24},{8,4},{16,12},{24,20},{5,9},{13,17},{21,25},... | collective-permute-start | bytes 393224 | tf_op jit(solution)/shard_map/ppermute | solution.py:238
  20.2 0.0 collective-permute-done.3.refs_4_
  20.2 0.0 copy-start.3
  20.3 3.4 %collective-permute-done.4.refs_5_ = f32[4,2,32,128]{3,2,1,0:T(8,128)S(1)} collective-permute-done((f32[4,2,32,128]{3,2,1,0:T(8,128)}, f32[4,2,32,128]{3,2,1,0:T(8,128)S(1)}, u32[]{:S(2)}, u32[]{:S(2)}) %collective-permute-start.4) | collective-permute-done | bytes 131104 | tf_op jit(solution)/shard_map/ppermute | solution.py:238
  23.6 0.0 copy-done.3
  23.6 0.0 copy-start.4
  23.6 0.6 %copy-done.4 = f32[4,2,32,128]{3,2,1,0:T(8,128)} copy-done((f32[4,2,32,128]{3,2,1,0:T(8,128)}, f32[4,2,32,128]{3,2,1,0:T(8,128)S(1)}, u32[]{:S(2)}) %copy-start.4) | copy-done | bytes 131096
  24.3 4.9 %steps_and_views.1 = (f32[8,8,128]{2,1,0:T(8,128)}, f32[8,8,128]{2,1,0:T(8,128)}, f32[4,4,8,32]{3,2,1,0:T(8,128)}) custom-call(f32[12]{0:T(128)} %ks_ref.1, f32[12]{0:T(128)} %alpha_ref.1, f32[4]{0:T(128)} %tilt_ref.1, f32[3]{0:T(128)} %gain_ref.1, f32[3]{0:T(128)} %middle_ref.1, s32[4,4]{1,0:T(4,128)} %rank_ref.1, f32[4,8,8,128]{3,2,1,0:T(8,128)} %pack.1.refs_0_, ...), custom_call_target="tpu_custom_call" | custom-call | tf_op jit(solution)/shard_map/steps_and_views/pallas_call | solution.py:242
Async XLA Ops:
  2.1 5.6 %collective-permute-start.2 = (f32[4,8,8,128]{3,2,1,0:T(8,128)}, f32[4,8,8,128]{3,2,1,0:T(8,128)S(1)}, u32[]{:S(2)}, u32[]{:S(2)}) collective-permute-start(f32[4,8,8,128]{3,2,1,0:T(8,128)} %pack.1.refs_0_), channel_id=1, source_target_pairs={{0,3},{1,0},{2,1},{3,2},{4,7},{5,4},{6,5},{7,6},{8,11},{9,8},{10,9... | collective-permute-start | bytes 393224 | tf_op jit(solution)/shard_map/ppermute | solution.py:225
  5.1 4.9 %collective-permute-start.1 = (f32[4,8,8,128]{3,2,1,0:T(8,128)}, f32[4,8,8,128]{3,2,1,0:T(8,128)S(1)}, u32[]{:S(2)}, u32[]{:S(2)}) collective-permute-start(f32[4,8,8,128]{3,2,1,0:T(8,128)} %pack.1.refs_0_), channel_id=1, source_target_pairs={{0,2},{1,3},{2,0},{3,1},{4,6},{5,7},{6,4},{7,5},{8,10},{9,11},{10,... | collective-permute-start | bytes 393224 | tf_op jit(solution)/shard_map/ppermute | solution.py:225
  5.3 5.9 %collective-permute-start = (f32[4,8,8,128]{3,2,1,0:T(8,128)}, f32[4,8,8,128]{3,2,1,0:T(8,128)S(1)}, u32[]{:S(2)}, u32[]{:S(2)}) collective-permute-start(f32[4,8,8,128]{3,2,1,0:T(8,128)} %pack.1.refs_0_), channel_id=1, source_target_pairs={{0,1},{1,2},{2,3},{3,0},{4,5},{5,6},{6,7},{7,4},{8,9},{9,10},{10,1... | collective-permute-start | bytes 393224 | tf_op jit(solution)/shard_map/ppermute | solution.py:225
  7.7 3.6 %copy-start = (f32[4,8,8,128]{3,2,1,0:T(8,128)}, f32[4,8,8,128]{3,2,1,0:T(8,128)S(1)}, u32[]{:S(2)}) copy-start(f32[4,8,8,128]{3,2,1,0:T(8,128)S(1)} %collective-permute-done.2.refs_3_) | copy-start | bytes 393220
  9.9 1.3 %copy-start.1 = (f32[4,8,8,128]{3,2,1,0:T(8,128)}, f32[4,8,8,128]{3,2,1,0:T(8,128)S(1)}, u32[]{:S(2)}) copy-start(f32[4,8,8,128]{3,2,1,0:T(8,128)S(1)} %collective-permute-done.1.refs_2_) | copy-start | bytes 393220
  11.2 0.7 %copy-start.2 = (f32[4,8,8,128]{3,2,1,0:T(8,128)}, f32[4,8,8,128]{3,2,1,0:T(8,128)S(1)}, u32[]{:S(2)}) copy-start(f32[4,8,8,128]{3,2,1,0:T(8,128)S(1)} %collective-permute-done.refs_1_) | copy-start | bytes 393220
  13.7 6.5 %collective-permute-start.3 = (f32[4,2,32,128]{3,2,1,0:T(8,128)}, f32[4,2,32,128]{3,2,1,0:T(8,128)S(1)}, u32[]{:S(2)}, u32[]{:S(2)}) collective-permute-start(f32[4,2,32,128]{3,2,1,0:T(8,128)} %get-tuple-element.5), channel_id=1, source_target_pairs={{0,4},{8,12},{16,20},{24,28},{4,0},{12,8},{20,16},{28,24},{1,5},{9... | collective-permute-start | bytes 393224 | tf_op jit(solution)/shard_map/ppermute | solution.py:239
  17.1 6.5 %collective-permute-start.4 = (f32[4,2,32,128]{3,2,1,0:T(8,128)}, f32[4,2,32,128]{3,2,1,0:T(8,128)S(1)}, u32[]{:S(2)}, u32[]{:S(2)}) collective-permute-start(f32[4,2,32,128]{3,2,1,0:T(8,128)} %get-tuple-element.6), channel_id=1, source_target_pairs={{4,8},{12,16},{20,24},{8,4},{16,12},{24,20},{5,9},{13,17},{21,25},... | collective-permute-start | bytes 393224 | tf_op jit(solution)/shard_map/ppermute | solution.py:238
  20.2 3.4 %copy-start.3 = (f32[4,2,32,128]{3,2,1,0:T(8,128)}, f32[4,2,32,128]{3,2,1,0:T(8,128)S(1)}, u32[]{:S(2)}) copy-start(f32[4,2,32,128]{3,2,1,0:T(8,128)S(1)} %collective-permute-done.3.refs_4_) | copy-start | bytes 393220
  23.6 0.6 %copy-start.4 = (f32[4,2,32,128]{3,2,1,0:T(8,128)}, f32[4,2,32,128]{3,2,1,0:T(8,128)S(1)}, u32[]{:S(2)}) copy-start(f32[4,2,32,128]{3,2,1,0:T(8,128)S(1)} %collective-permute-done.4.refs_5_) | copy-start | bytes 393220

commit v2 on v1

--- a/solution.py
+++ b/solution.py
@@ -11,15 +11,26 @@
 IMPEDANCE = 4.0
 DIFFUSE = 0.12
 
+MIB = 1 << 20
 VMEM = pl.BlockSpec(memory_space=pltpu.VMEM)
+HBM = pl.BlockSpec(memory_space=pltpu.HBM)
 SMEM = pl.BlockSpec(memory_space=pltpu.SMEM)
 
 
-def pack_kernel(head_ref, temp_ref, soil_ref, ice_ref, out_ref):
-    out_ref[0] = head_ref[...]
-    out_ref[1] = temp_ref[...]
-    out_ref[2] = soil_ref[...].astype(jnp.float32)
-    out_ref[3] = ice_ref[...].astype(jnp.float32)
+def pack_kernel(head_ref, temp_ref, soil_ref, ice_ref, out_ref, whole_ref, sems):
+    copies = [
+        pltpu.make_async_copy(soil_ref, whole_ref.at[0], sems.at[0]),
+        pltpu.make_async_copy(ice_ref, whole_ref.at[1], sems.at[1]),
+        pltpu.make_async_copy(head_ref, out_ref.at[0], sems.at[2]),
+        pltpu.make_async_copy(temp_ref, out_ref.at[1], sems.at[3]),
+    ]
+    for copy in copies:
+        copy.start()
+    for field in range(2):
+        copies[field].wait()
+        out_ref[2 + field] = whole_ref[field].astype(jnp.float32)
+    for copy in copies[2:]:
+        copy.wait()
 
 
 def column_of(peer, count, cols):
@@ -215,10 +226,15 @@
     packed = pl.pallas_call(
         pack_kernel,
         out_shape=jax.ShapeDtypeStruct((4, rows, cols, depth), jnp.float32),
-        in_specs=[VMEM] * 4,
+        in_specs=[HBM] * 4,
         out_specs=VMEM,
+        scratch_shapes=[
+            pltpu.VMEM((2, rows, cols, depth), jnp.int32),
+            pltpu.SemaphoreType.DMA((4,)),
+        ],
+        compiler_params=pltpu.CompilerParams(vmem_limit_bytes=8 * MIB),
         name="pack",
-    )(head, warmth, soil, icebound)
+    )(*(pltpu.with_memory_space_constraint(x, pltpu.HBM) for x in (head, warmth, soil, icebound)))
     blocks = [packed]
     for peer in range(1, count):
         ring = [(i, (i + peer) % count) for i in range(count)]
@@ -230,13 +246,14 @@
         out_shape=(border, border),
         in_specs=[VMEM] * count,
         out_specs=(VMEM, VMEM),
+        compiler_params=pltpu.CompilerParams(vmem_limit_bytes=8 * MIB),
         name="edges",
     )(*blocks)
     pairs = [(i, i + 1) for i in range(rows_count - 1)]
     pairs = [pairs[0::2], pairs[1::2]]
     pairs = [p + [(b, a) for a, b in p] for p in pairs]
+    inner = lax.ppermute(inner, "gx", pairs[0])
     outer = lax.ppermute(outer, "gx", pairs[1])
-    inner = lax.ppermute(inner, "gx", pairs[0])
 
     cell = jax.ShapeDtypeStruct((rows, cols, depth), jnp.float32)
     return pl.pallas_call(
@@ -252,6 +269,7 @@
             pltpu.VMEM((4, rows + 2 * STEPS, width, depth), jnp.float32),
             pltpu.VMEM((rows * width, depth), jnp.float32),
         ],
+        compiler_params=pltpu.CompilerParams(vmem_limit_bytes=24 * MIB),
         name="steps_and_views",
     )(ks, alpha, tilt, gain, middle, ranks, *blocks, inner, outer)
 

time: 29.4 us -> 24.2 us (0.82)
  Pallas kernels: 8.19 us -> 5.18 us
  local copies, waits for them, and re-layouts: 1.33 us -> 0.03 us
  starting transfers between devices: 10 us -> 9.55 us
  waiting for transfers between devices: 8.98 us -> 8.55 us
    pallas_call x1, Pallas kernels: 1.81 us -> 0.02 us  [shards(): pl.pallas_call(functools.partial(edge_kernel, count), out_shape=(border,...]
    unnamed x10 -> x12, local copies, waits for them, and re-layouts: 1.33 us -> 0.03 us
    pallas_call x1, Pallas kernels: 1.46 us -> 0.84 us  [shards(): pl.pallas_call(pack_kernel, out_shape=jax.ShapeDtypeStruct((4, rows, cols...]
    pallas_call x1, Pallas kernels: 4.92 us -> 4.32 us  [shards(): pl.pallas_call(functools.partial(main_kernel, count, rows_count), out_sha...]
    ppermute x1, starting transfers between devices: 3.43 us -> 2.87 us  [shards(): inner = lax.ppermute(inner, 'gx', pairs[0])]
where the time goes in v2:
time: 24.2 us; the launch traced here: 24 us
  starting transfers between devices  9.55 us (39%)
  waiting for transfers between devices  8.55 us (35%)
  Pallas kernels  5.18 us (21%)
  between operations  0.72 us (3%)
    ppermute x3, waiting for transfers between devices, shards(): blocks.append(lax.ppermute(packed, 'gy', ring))  5.39 us
    pallas_call x1, Pallas kernels, shards(): pl.pallas_call(functools.partial(main_kernel, count, rows_count), out_sha...  4.32 us
    ppermute x3, starting transfers between devices, shards(): blocks.append(lax.ppermute(packed, 'gy', ring))  3.58 us
    ppermute x1, waiting for transfers between devices, shards(): outer = lax.ppermute(outer, 'gx', pairs[1])  3.15 us
    ppermute x1, starting transfers between devices, shards(): outer = lax.ppermute(outer, 'gx', pairs[1])  3.1 us
    ppermute x1, starting transfers between devices, shards(): inner = lax.ppermute(inner, 'gx', pairs[0])  2.87 us
    pallas_call x1, Pallas kernels, shards(): pl.pallas_call(pack_kernel, out_shape=jax.ShapeDtypeStruct((4, rows, cols...  0.84 us
  transfers between devices with their start and end apart: 5, of which 4 were waited for; matrix products, arithmetic and copies ran while one was open for 0% of the time, Pallas kernels for 0%

profile of v2, /device:TPU:1, one launch (start us, length us, event | category | flops | bytes accessed | tf_op | source)
XLA Modules:
  0.0 24.0 jit_solution(14089111415976998805)
XLA Ops:
  0.6 0.8 %pack.1.refs_0_ = f32[4,8,8,128]{3,2,1,0:T(8,128)S(1)} custom-call(f32[8,8,128]{2,1,0:T(8,128)} %head_ref.1, f32[8,8,128]{2,1,0:T(8,128)} %temp_ref.1, s32[8,8,128]{2,1,0:T(8,128)} %soil_ref.1, s32[8,8,128]{2,1,0:T(8,128)} %ice_ref.1), custom_call_target="tpu_custom_call" | custom-call | tf_op jit(solution)/shard_map/pack/pallas_call | solution.py:226
  1.5 3.0 %collective-permute-start.2 = (f32[4,8,8,128]{3,2,1,0:T(8,128)S(1)}, f32[4,8,8,128]{3,2,1,0:T(8,128)S(1)}, u32[]{:S(2)}, u32[]{:S(2)}) collective-permute-start(f32[4,8,8,128]{3,2,1,0:T(8,128)S(1)} %pack.1.refs_0_), channel_id=1, source_target_pairs={{0,3},{1,0},{2,1},{3,2},{4,7},{5,4},{6,5},{7,6},{8,11},{9,8},{10,9... | collective-permute-start | bytes 393224 | tf_op jit(solution)/shard_map/ppermute | solution.py:241
  4.5 0.2 collective-permute-start.1
  4.7 0.3 %collective-permute-start = (f32[4,8,8,128]{3,2,1,0:T(8,128)S(1)}, f32[4,8,8,128]{3,2,1,0:T(8,128)S(1)}, u32[]{:S(2)}, u32[]{:S(2)}) collective-permute-start(f32[4,8,8,128]{3,2,1,0:T(8,128)S(1)} %pack.1.refs_0_), channel_id=1, source_target_pairs={{0,1},{1,2},{2,3},{3,0},{4,5},{5,6},{6,7},{7,4},{8,9},{9,10},{10,1... | collective-permute-start | bytes 393224 | tf_op jit(solution)/shard_map/ppermute | solution.py:241
  5.1 1.7 %collective-permute-done.2.refs_3_ = f32[4,8,8,128]{3,2,1,0:T(8,128)S(1)} collective-permute-done((f32[4,8,8,128]{3,2,1,0:T(8,128)S(1)}, f32[4,8,8,128]{3,2,1,0:T(8,128)S(1)}, u32[]{:S(2)}, u32[]{:S(2)}) %collective-permute-start.2) | collective-permute-done | bytes 131104 | tf_op jit(solution)/shard_map/ppermute | solution.py:241
  6.8 2.4 %collective-permute-done.1.refs_2_ = f32[4,8,8,128]{3,2,1,0:T(8,128)S(1)} collective-permute-done((f32[4,8,8,128]{3,2,1,0:T(8,128)S(1)}, f32[4,8,8,128]{3,2,1,0:T(8,128)S(1)}, u32[]{:S(2)}, u32[]{:S(2)}) %collective-permute-start.1) | collective-permute-done | bytes 131104 | tf_op jit(solution)/shard_map/ppermute | solution.py:241
  9.2 1.3 %collective-permute-done.refs_1_ = f32[4,8,8,128]{3,2,1,0:T(8,128)S(1)} collective-permute-done((f32[4,8,8,128]{3,2,1,0:T(8,128)S(1)}, f32[4,8,8,128]{3,2,1,0:T(8,128)S(1)}, u32[]{:S(2)}, u32[]{:S(2)}) %collective-permute-start) | collective-permute-done | bytes 131104 | tf_op jit(solution)/shard_map/ppermute | solution.py:241
  10.5 0.0 copy-start.4
  10.5 0.0 copy-start.5
  10.5 0.0 copy-start
  10.5 0.0 copy-start.1
  10.5 0.0 copy-start.2
  10.5 0.0 copy-start.3
  10.5 2.9 %collective-permute-start.3 = (f32[4,2,32,128]{3,2,1,0:T(8,128)S(1)}, f32[4,2,32,128]{3,2,1,0:T(8,128)S(1)}, u32[]{:S(2)}, u32[]{:S(2)}) collective-permute-start(f32[4,2,32,128]{3,2,1,0:T(8,128)S(1)} %get-tuple-element.5), channel_id=1, source_target_pairs={{0,4},{8,12},{16,20},{24,28},{4,0},{12,8},{20,16},{28,24},{1,5},{9... | collective-permute-start | bytes 393224 | tf_op jit(solution)/shard_map/ppermute | solution.py:255
  13.4 3.1 %collective-permute-start.4 = (f32[4,2,32,128]{3,2,1,0:T(8,128)S(1)}, f32[4,2,32,128]{3,2,1,0:T(8,128)S(1)}, u32[]{:S(2)}, u32[]{:S(2)}) collective-permute-start(f32[4,2,32,128]{3,2,1,0:T(8,128)S(1)} %get-tuple-element.6), channel_id=1, source_target_pairs={{4,8},{12,16},{20,24},{8,4},{16,12},{24,20},{5,9},{13,17},{21,25},... | collective-permute-start | bytes 393224 | tf_op jit(solution)/shard_map/ppermute | solution.py:256
  16.5 0.0 collective-permute-done.3.refs_4_
  16.5 3.2 %collective-permute-done.4.refs_5_ = f32[4,2,32,128]{3,2,1,0:T(8,128)S(1)} collective-permute-done((f32[4,2,32,128]{3,2,1,0:T(8,128)S(1)}, f32[4,2,32,128]{3,2,1,0:T(8,128)S(1)}, u32[]{:S(2)}, u32[]{:S(2)}) %collective-permute-start.4) | collective-permute-done | bytes 131104 | tf_op jit(solution)/shard_map/ppermute | solution.py:256
  19.7 0.0 copy-done.4
  19.7 0.0 copy-done.5
  19.7 0.0 copy-done
  19.7 0.0 copy-done.1
  19.7 0.0 copy-done.2
  19.7 0.0 copy-done.3
  19.7 4.3 %steps_and_views.1 = (f32[8,8,128]{2,1,0:T(8,128)}, f32[8,8,128]{2,1,0:T(8,128)}, f32[4,4,8,32]{3,2,1,0:T(8,128)}) custom-call(f32[12]{0:T(128)S(1)} %copy-done.1, f32[12]{0:T(128)S(1)} %copy-done.2, f32[4]{0:T(128)S(1)} %copy-done.3, f32[3]{0:T(128)S(1)} %copy-done.4, f32[3]{0:T(128)S(1)} %copy-done.5, s32[4,4]{1,0:T(4,128)S(1)} %copy-done, ...), custom_call_target="tpu_custom_call" | custom-call | tf_op jit(solution)/shard_map/steps_and_views/pallas_call | solution.py:259
  (1 shorter events, 0.0 us)
Async XLA Ops:
  1.5 5.3 %collective-permute-start.2 = (f32[4,8,8,128]{3,2,1,0:T(8,128)S(1)}, f32[4,8,8,128]{3,2,1,0:T(8,128)S(1)}, u32[]{:S(2)}, u32[]{:S(2)}) collective-permute-start(f32[4,8,8,128]{3,2,1,0:T(8,128)S(1)} %pack.1.refs_0_), channel_id=1, source_target_pairs={{0,3},{1,0},{2,1},{3,2},{4,7},{5,4},{6,5},{7,6},{8,11},{9,8},{10,9... | collective-permute-start | bytes 393224 | tf_op jit(solution)/shard_map/ppermute | solution.py:241
  4.5 4.6 %collective-permute-start.1 = (f32[4,8,8,128]{3,2,1,0:T(8,128)S(1)}, f32[4,8,8,128]{3,2,1,0:T(8,128)S(1)}, u32[]{:S(2)}, u32[]{:S(2)}) collective-permute-start(f32[4,8,8,128]{3,2,1,0:T(8,128)S(1)} %pack.1.refs_0_), channel_id=1, source_target_pairs={{0,2},{1,3},{2,0},{3,1},{4,6},{5,7},{6,4},{7,5},{8,10},{9,11},{10,... | collective-permute-start | bytes 393224 | tf_op jit(solution)/shard_map/ppermute | solution.py:241
  4.7 5.7 %collective-permute-start = (f32[4,8,8,128]{3,2,1,0:T(8,128)S(1)}, f32[4,8,8,128]{3,2,1,0:T(8,128)S(1)}, u32[]{:S(2)}, u32[]{:S(2)}) collective-permute-start(f32[4,8,8,128]{3,2,1,0:T(8,128)S(1)} %pack.1.refs_0_), channel_id=1, source_target_pairs={{0,1},{1,2},{2,3},{3,0},{4,5},{5,6},{6,7},{7,4},{8,9},{9,10},{10,1... | collective-permute-start | bytes 393224 | tf_op jit(solution)/shard_map/ppermute | solution.py:241
  10.5 9.2 %copy-start.4 = (f32[3]{0:T(128)S(1)}, f32[3]{0:T(128)}, u32[]{:S(2)}) copy-start(f32[3]{0:T(128)} %gain_ref.1) | copy-start | bytes 40
  10.5 9.2 %copy-start.5 = (f32[3]{0:T(128)S(1)}, f32[3]{0:T(128)}, u32[]{:S(2)}) copy-start(f32[3]{0:T(128)} %middle_ref.1) | copy-start | bytes 40
  10.5 9.2 %copy-start = (s32[4,4]{1,0:T(4,128)S(1)}, s32[4,4]{1,0:T(4,128)}, u32[]{:S(2)}) copy-start(s32[4,4]{1,0:T(4,128)} %rank_ref.1) | copy-start | bytes 196
  10.5 9.2 %copy-start.1 = (f32[12]{0:T(128)S(1)}, f32[12]{0:T(128)}, u32[]{:S(2)}) copy-start(f32[12]{0:T(128)} %ks_ref.1) | copy-start | bytes 148
  10.5 9.2 %copy-start.2 = (f32[12]{0:T(128)S(1)}, f32[12]{0:T(128)}, u32[]{:S(2)}) copy-start(f32[12]{0:T(128)} %alpha_ref.1) | copy-start | bytes 148
  10.5 9.2 %copy-start.3 = (f32[4]{0:T(128)S(1)}, f32[4]{0:T(128)}, u32[]{:S(2)}) copy-start(f32[4]{0:T(128)} %tilt_ref.1) | copy-start | bytes 52
  10.5 6.0 %collective-permute-start.3 = (f32[4,2,32,128]{3,2,1,0:T(8,128)S(1)}, f32[4,2,32,128]{3,2,1,0:T(8,128)S(1)}, u32[]{:S(2)}, u32[]{:S(2)}) collective-permute-start(f32[4,2,32,128]{3,2,1,0:T(8,128)S(1)} %get-tuple-element.5), channel_id=1, source_target_pairs={{0,4},{8,12},{16,20},{24,28},{4,0},{12,8},{20,16},{28,24},{1,5},{9... | collective-permute-start | bytes 393224 | tf_op jit(solution)/shard_map/ppermute | solution.py:255
  13.4 6.3 %collective-permute-start.4 = (f32[4,2,32,128]{3,2,1,0:T(8,128)S(1)}, f32[4,2,32,128]{3,2,1,0:T(8,128)S(1)}, u32[]{:S(2)}, u32[]{:S(2)}) collective-permute-start(f32[4,2,32,128]{3,2,1,0:T(8,128)S(1)} %get-tuple-element.6), channel_id=1, source_target_pairs={{4,8},{12,16},{20,24},{8,4},{16,12},{24,20},{5,9},{13,17},{21,25},... | collective-permute-start | bytes 393224 | tf_op jit(solution)/shard_map/ppermute | solution.py:256

commit v3 on v2

v3 whole, which is shorter than its diff:
```python
import functools

import jax
import jax.numpy as jnp
from jax import lax
from jax.experimental import pallas as pl
from jax.experimental.pallas import tpu as pltpu
from jax.sharding import PartitionSpec as P

STEPS = 2
IMPEDANCE = 4.0
DIFFUSE = 0.12
SUB = 8

MIB = 1 << 20
VMEM = pl.BlockSpec(memory_space=pltpu.VMEM)
HBM = pl.BlockSpec(memory_space=pltpu.HBM)
SMEM = pl.BlockSpec(memory_space=pltpu.SMEM)


def f32(*shape):
    return jax.ShapeDtypeStruct(shape, jnp.float32)


def params(mib):
    return pltpu.CompilerParams(vmem_limit_bytes=mib * MIB)


def halves_fit(count, rows, cols, depth):
    width, strip, half = count * cols, depth // count, cols // 2
    if count < 3 or cols != SUB or rows % SUB or width % 2 or SUB % STEPS:
        return False

    def seen(y):
        return strip + 2 * (abs(y - width // 2) + STEPS)

    starts = [q * cols + plane for q in range(count) for plane in range(half)]
    return all(seen(y) + seen(y + half) <= depth for y in starts)


def pack_kernel(count, packed, head_ref, temp_ref, soil_ref, ice_ref, own_ref, *refs):
    sent_refs, (whole_ref, sems) = refs[:-2], refs[-2:]
    rows, cols, depth = own_ref.shape[1:]
    copies = [
        pltpu.make_async_copy(soil_ref, whole_ref.at[0], sems.at[0]),
        pltpu.make_async_copy(ice_ref, whole_ref.at[1], sems.at[1]),
        pltpu.make_async_copy(head_ref, own_ref.at[0], sems.at[2]),
        pltpu.make_async_copy(temp_ref, own_ref.at[1], sems.at[3]),
    ]
    for copy in copies:
        copy.start()
    if packed:
        gy = lax.axis_index("gy")
        strip, half = depth // count, cols // 2
        sub = lax.broadcasted_iota(jnp.int32, (SUB, depth), 0)
        lane = lax.broadcasted_iota(jnp.int32, (SUB, depth), 1)
        reach = jnp.abs(gy * cols + lax.rem(sub, half) - count * cols // 2) + STEPS
        upper = sub < half
        seen = []
        for peer in range(1, count):
            begin = lax.rem(gy + peer, count) * strip - reach
            seen.append(((lane - begin) & (depth - 1)) < strip + 2 * reach)
    for field in (2, 3, 0, 1):
        copies[field - 2 if field > 1 else field + 2].wait()
        if field > 1:
            own_ref[field] = whole_ref[field - 2].astype(jnp.float32)
        if not packed:
            continue
        for row in range(0, rows, 2):
            a, b = own_ref[field, row], own_ref[field, row + 1]
            first = jnp.where(upper, a, pltpu.roll(b, half, 0))
            second = jnp.where(upper, pltpu.roll(a, half, 0), b)
            second = pltpu.roll(second, depth // 2, 1)
            for peer in range(1, count):
                at = pl.ds(row * half, SUB)
                sent_refs[peer - 1][field, at, :] = jnp.where(seen[peer - 1], first, second)
        for row in range(rows):
            at = pl.ds(rows * half + row * STEPS, STEPS)
            sent_refs[0][field, at, :] = own_ref[field, row, cols - STEPS :, :]
            sent_refs[count - 2][field, at, :] = own_ref[field, row, :STEPS, :]


def read_row(count, packed, rows, block, peer, field, row):
    if not packed or peer == 0:
        return block[field, row]
    depth = block.shape[-1]
    half = SUB // 2
    sub = lax.broadcasted_iota(jnp.int32, (SUB, depth), 0)
    near = block[field, row // 2 * SUB : row // 2 * SUB + SUB]
    far = pltpu.roll(near, depth // 2, 1)
    if row % 2:
        near = pltpu.roll(near, half, 0)
    else:
        far = pltpu.roll(far, half, 0)
    value = jnp.where(sub < half, near, far)
    if peer in (1, count - 1):
        each = SUB // STEPS
        begin = rows * half + row // each * SUB
        border = block[field, begin : begin + SUB]
        place = SUB - STEPS if peer == 1 else 0
        move = (place - row % each * STEPS) % SUB
        border = pltpu.roll(border, move, 0) if move else border
        keep = sub >= SUB - STEPS if peer == 1 else sub < STEPS
        value = jnp.where(keep, border, value)
    return value


def columns_of(peer, count, cols):
    at = lax.rem(lax.axis_index("gy") - peer + count, count)
    return pl.ds(pl.multiple_of(at * cols, cols), cols)


def edge_kernel(count, packed, *refs):
    blocks, (inner_ref, outer_ref) = refs[:count], refs[count:]
    rows, cols = blocks[0].shape[1:3]
    odd = lax.rem(lax.axis_index("gx"), 2) == 1
    for peer, block in enumerate(blocks):
        at = columns_of(peer, count, cols)
        for field in range(4):
            for row in range(STEPS):
                low = read_row(count, packed, rows, block, peer, field, row)
                high = read_row(count, packed, rows, block, peer, field, rows - STEPS + row)
                inner_ref[field, row, at, :] = jnp.where(odd, low, high)
                outer_ref[field, row, at, :] = jnp.where(odd, high, low)


def conductivity(head, temp, ks, alpha, ice):
    frozen = (0.5 * IMPEDANCE) * ice * (1.0 - jnp.tanh(temp))
    return 0.5 * ks * jnp.exp(alpha * jnp.minimum(head, 0.0) - frozen)


class Plane:
    def __init__(self, width, depth, ks_ref, alpha_ref):
        self.width, self.depth = width, depth
        lane = lax.broadcasted_iota(jnp.int32, (width, depth), 1)
        col = lax.broadcasted_iota(jnp.int32, (width, depth), 0)
        self.up_open, self.down_open = lane < depth - 1, lane > 0
        self.next_open, self.last_open = col < width - 1, col > 0
        self.tables = []
        for table_ref in (ks_ref, alpha_ref):
            table = jnp.zeros((width, depth), jnp.float32)
            for number in range(table_ref.shape[0]):
                table = jnp.where(lane == number, table_ref[number], table)
            self.tables.append(table)

    def soil(self, index):
        index = index.astype(jnp.int32)
        return [
            jnp.take_along_axis(t, index, axis=1, mode="promise_in_bounds") for t in self.tables
        ]

    def within(self, head, k):
        flux = (k + pltpu.roll(k, self.width - 1, 0)) * (
            pltpu.roll(head, self.width - 1, 0) - head
        )
        flux = jnp.where(self.next_open, flux, 0.0)
        change = flux - pltpu.roll(flux, 1, 0)
        flux = (k + pltpu.roll(k, self.depth - 1, 1)) * (
            pltpu.roll(head, self.depth - 1, 1) - head + 1.0
        )
        flux = jnp.where(self.up_open, flux, 0.0)
        return change + (flux - pltpu.roll(flux, 1, 1))

    def near(self, t):
        total = jnp.where(self.next_open, pltpu.roll(t, self.width - 1, 0), 0.0)
        total = total + jnp.where(self.last_open, pltpu.roll(t, 1, 0), 0.0)
        total = total + jnp.where(self.up_open, pltpu.roll(t, self.depth - 1, 1), 0.0)
        return total + jnp.where(self.down_open, pltpu.roll(t, 1, 1), 0.0)


def across(k_a, head_a, k_b, head_b):
    return (k_a + k_b) * (head_b - head_a)


def middle_kernel(count, packed, ks_ref, alpha_ref, *refs):
    blocks, (head_ref, temp_ref, rim_ref, all_ref) = refs[:count], refs[count:]
    rows, cols, depth = blocks[0].shape[1:]
    plane = Plane(count * cols, depth, ks_ref, alpha_ref)
    for peer, block in enumerate(blocks):
        at = columns_of(peer, count, cols)
        for field in range(4):
            for row in range(rows):
                all_ref[field, row, at, :] = read_row(
                    count, packed, rows, block, peer, field, row
                )
    last = rows - 1
    head, temp, k, soil = [], [], [], []
    for row in range(rows):
        head.append(all_ref[0, row])
        temp.append(all_ref[1, row])
        soil.append((*plane.soil(all_ref[2, row]), all_ref[3, row]))
        k.append(conductivity(head[row], temp[row], *soil[row]))
    for side, row in ((0, 0), (1, last)):
        for number, value in enumerate((head[row], temp[row], k[row], *soil[row])):
            rim_ref[side, number] = value
    for step in range(STEPS):
        first, end = step, last - step
        fluxes = {
            row: across(k[row], head[row], k[row + 1], head[row + 1]) for row in range(first, end)
        }
        new_head, new_temp = {}, {}
        for row in range(first, end + 1):
            change, near = plane.within(head[row], k[row]), plane.near(temp[row])
            if row < end:
                change, near = change + fluxes[row], near + temp[row + 1]
            if row > first:
                change, near = change - fluxes[row - 1], near + temp[row - 1]
            new_head[row] = head[row] + change
            new_temp[row] = temp[row] + DIFFUSE * (near - 6.0 * temp[row])
        final = range(first, end + 1) if step == STEPS - 1 else (first, end)
        for row in final:
            head_ref[row] = new_head[row]
            temp_ref[row] = new_temp[row]
        if step == STEPS - 1:
            break
        head, temp = new_head, new_temp
        k = {r: conductivity(head[r], temp[r], *soil[r]) for r in range(first + 1, end)}
        for side, row in ((0, first + 1), (1, end - 1)):
            for number, value in enumerate((head[row], temp[row], k[row])):
                rim_ref[side, 6 + number] = value


def scalar_floor(x):
    whole = x.astype(jnp.int32)
    return whole - (whole.astype(jnp.float32) > x).astype(jnp.int32)


def last_kernel(
    count,
    rows_count,
    cols,
    ks_ref,
    alpha_ref,
    tilt_from,
    gain_from,
    middle_from,
    rank_from,
    inner_ref,
    outer_ref,
    base_head_ref,
    base_temp_ref,
    rim_ref,
    head_out_ref,
    temp_out_ref,
    image_ref,
    head_ref,
    temp_ref,
    theta_ref,
    tilt_ref,
    gain_ref,
    middle_ref,
    rank_ref,
    sems,
):
    rows, width, depth = base_head_ref.shape
    strip = depth // count
    views = tilt_ref.shape[0]
    scalars = [
        pltpu.make_async_copy(tilt_from, tilt_ref, sems.at[2]),
        pltpu.make_async_copy(gain_from, gain_ref, sems.at[3]),
        pltpu.make_async_copy(middle_from, middle_ref, sems.at[4]),
        pltpu.make_async_copy(rank_from, rank_ref, sems.at[5]),
    ]
    for copy in scalars:
        copy.start()
    gx = lax.axis_index("gx")
    gy = lax.axis_index("gy")
    odd = lax.rem(gx, 2)
    plane = Plane(width, depth, ks_ref, alpha_ref)

    for row in range(STEPS, rows - STEPS):
        head_ref[row] = base_head_ref[row]
        temp_ref[row] = base_temp_ref[row]
    for halo_ref, side in ((inner_ref, 1 - odd), (outer_ref, odd)):
        there = jnp.where(side == 0, gx > 0, gx < rows_count - 1).astype(jnp.float32)
        near, far = 1 - side, side
        head_n, temp_n, soil_n, ice_n = [halo_ref[field, near] for field in range(4)]
        head_f, temp_f, soil_f, ice_f = [halo_ref[field, far] for field in range(4)]
        soil_n = (*plane.soil(soil_n), ice_n)
        soil_f = (*plane.soil(soil_f), ice_f)
        k_n = conductivity(head_n, temp_n, *soil_n)
        k_f = conductivity(head_f, temp_f, *soil_f)
        head_e, temp_e, k_e = [rim_ref[side, number] for number in range(3)]
        soil_e = [rim_ref[side, number] for number in range(3, 6)]
        head_i, temp_i, k_i = [rim_ref[side, number] for number in range(6, 9)]
        row_e = side * (rows - 1)
        row_i = 1 + side * (rows - 3)

        flux = across(k_n, head_n, k_e, head_e)
        change = flux + across(k_n, head_n, k_f, head_f) + plane.within(head_n, k_n)
        total = temp_e + temp_f + plane.near(temp_n)
        temp_1 = there * (temp_n + DIFFUSE * (total - 6.0 * temp_n))
        head_1 = head_n + change
        k_1 = conductivity(head_1, temp_1, *soil_n)
        head_e = base_head_ref[row_e] - there * flux
        temp_e = base_temp_ref[row_e] + DIFFUSE * (there * temp_n)
        k_e = conductivity(head_e, temp_e, *soil_e)
        flux = across(k_e, head_e, k_i, head_i)
        change = flux + there * across(k_e, head_e, k_1, head_1) + plane.within(head_e, k_e)
        total = temp_1 + temp_i + plane.near(temp_e)
        head_ref[row_e] = head_e + change
        temp_ref[row_e] = temp_e + DIFFUSE * (total - 6.0 * temp_e)
        head_ref[row_i] = base_head_ref[row_i] - flux
        temp_ref[row_i] = base_temp_ref[row_i] + DIFFUSE * temp_e

    own = pl.ds(pl.multiple_of(gy * cols, cols), cols)
    copies = [
        pltpu.make_async_copy(head_ref.at[:, own, :], head_out_ref, sems.at[0]),
        pltpu.make_async_copy(temp_ref.at[:, own, :], temp_out_ref, sems.at[1]),
    ]
    for copy in copies:
        copy.start()
    for row in range(rows):
        theta = 0.05 + 0.4 * jnp.exp(0.8 * jnp.minimum(head_ref[row], 0.0))
        theta_ref[row * width : (row + 1) * width] = theta
    for copy in scalars:
        copy.wait()

    lane = lax.broadcasted_iota(jnp.int32, (rows, depth), 1)
    slab_of = lane // strip
    begin = gy * strip
    clear = [jnp.ones((rows, depth), jnp.float32) for _ in range(views)]
    thick = [jnp.zeros((rows, depth), jnp.float32) for _ in range(views)]
    shade = [[jnp.zeros((rows, depth), jnp.float32)] * 3 for _ in range(views)]
    for place in range(cols):
        layers = []
        for slab in range(count):
            y = slab * cols + place
            value = theta_ref[pl.ds(y, rows, stride=width), :]
            layers.append((value, pltpu.roll(value, depth - 1, 1) - value))
        for view in range(views):
            sample = None
            for slab in range(count):
                y = slab * cols + place
                shift = tilt_ref[view] * jnp.float32(y - 0.5 * width)
                turns = scalar_floor(shift * (1.0 / depth))
                wrapped = shift - depth * turns.astype(jnp.float32)
                base = scalar_floor(wrapped)
                frac = wrapped - base.astype(jnp.float32)
                value, rise = layers[slab]
                move = (slab * strip - begin - base) & (depth - 1)
                moved = pltpu.roll(value + frac * rise, move, 1)
                sample = moved if slab == 0 else jnp.where(slab_of == slab, moved, sample)
            tau = sample * (8.0 / width)
            thick[view] = thick[view] + tau
            rest = clear[view] * jnp.exp(-tau)
            weight = 0.5 * (clear[view] - rest)
            clear[view] = rest
            for c in range(3):
                glow = jnp.tanh((0.5 * gain_ref[c]) * (sample - middle_ref[c]))
                shade[view][c] = shade[view][c] + (weight + weight * glow)

    def over_slabs(x):
        size = strip
        while size < depth:
            x = x + pltpu.roll(x, size, 1)
            size *= 2
        return x

    for view in range(views):
        rank = jnp.zeros((rows, depth), jnp.int32)
        for slab in range(count):
            rank = jnp.where(slab_of == slab, rank_ref[view, slab], rank)
        front = jnp.zeros((rows, depth), jnp.float32)
        for d in range(1, count):
            nearer = pltpu.roll(rank, d * strip, 1) < rank
            front = front + jnp.where(nearer, pltpu.roll(thick[view], d * strip, 1), 0.0)
        through = jnp.exp(-front)
        for c in range(3):
            image_ref[view, c] = over_slabs(through * shade[view][c])[:, :strip]
        image_ref[view, 3] = (1.0 - jnp.exp(-over_slabs(thick[view])))[:, :strip]
    for copy in copies:
        copy.wait()


def shards(head, warmth, soil, icebound, ks, alpha, tilt, gain, middle, ranks):
    rows, cols, depth = head.shape
    count = lax.axis_size("gy")
    rows_count = lax.axis_size("gx")
    width = count * cols
    views = tilt.shape[0]
    assert depth & (depth - 1) == 0 and depth % count == 0
    assert count & (count - 1) == 0 and ranks.shape[1] == count
    packed = halves_fit(count, rows, cols, depth)

    sent = []
    if packed:
        for peer in range(1, count):
            more = STEPS if peer in (1, count - 1) else 0
            sent.append(f32(4, rows * (cols // 2 + more), depth))
    fields = [
        pltpu.with_memory_space_constraint(x, pltpu.HBM) for x in (head, warmth, soil, icebound)
    ]
    own, *sent = pl.pallas_call(
        functools.partial(pack_kernel, count, packed),
        out_shape=(f32(4, rows, cols, depth), *sent),
        in_specs=[HBM] * 4,
        out_specs=(VMEM,) * (1 + len(sent)),
        scratch_shapes=[
            pltpu.VMEM((2, rows, cols, depth), jnp.int32),
            pltpu.SemaphoreType.DMA((4,)),
        ],
        compiler_params=params(8),
        name="pack",
    )(*fields)
    blocks = [own]
    for peer in range(1, count):
        ring = [(i, (i + peer) % count) for i in range(count)]
        blocks.append(lax.ppermute(sent[peer - 1] if packed else own, "gy", ring))

    border = f32(4, STEPS, width, depth)
    inner, outer = pl.pallas_call(
        functools.partial(edge_kernel, count, packed),
        out_shape=(border, border),
        in_specs=[VMEM] * count,
        out_specs=(VMEM, VMEM),
        compiler_params=params(8),
        name="edges",
    )(*blocks)
    pairs = [(i, i + 1) for i in range(rows_count - 1)]
    pairs = [pairs[0::2], pairs[1::2]]
    pairs = [p + [(b, a) for a, b in p] for p in pairs]
    outer = lax.ppermute(outer, "gx", pairs[1])
    inner = lax.ppermute(inner, "gx", pairs[0])

    all_cells = f32(rows, width, depth)
    base_head, base_temp, rim = pl.pallas_call(
        functools.partial(middle_kernel, count, packed),
        out_shape=(all_cells, all_cells, f32(2, 9, width, depth)),
        in_specs=[SMEM] * 2 + [VMEM] * count,
        out_specs=(VMEM,) * 3,
        scratch_shapes=[pltpu.VMEM((4, rows, width, depth), jnp.float32)],
        compiler_params=params(16),
        name="within",
    )(ks, alpha, *blocks)

    cell = f32(rows, cols, depth)
    scalars = [
        pltpu.with_memory_space_constraint(x, pltpu.HBM) for x in (tilt, gain, middle, ranks)
    ]
    return pl.pallas_call(
        functools.partial(last_kernel, count, rows_count, cols),
        out_shape=(cell, cell, f32(views, 4, rows, depth // count)),
        in_specs=[SMEM] * 2 + [HBM] * 4 + [VMEM] * 5,
        out_specs=(HBM, HBM, VMEM),
        scratch_shapes=[
            pltpu.VMEM((rows, width, depth), jnp.float32),
            pltpu.VMEM((rows, width, depth), jnp.float32),
            pltpu.VMEM((rows * width, depth), jnp.float32),
            *(pltpu.SMEM(x.shape, x.dtype) for x in (tilt, gain, middle, ranks)),
            pltpu.SemaphoreType.DMA((6,)),
        ],
        compiler_params=params(16),
        name="views",
    )(ks, alpha, *scalars, inner, outer, base_head, base_temp, rim)


def solution(mesh):
    cells = P("gx", "gy", None)
    return jax.shard_map(
        shards,
        mesh=mesh,
        in_specs=(cells,) * 4 + (P(),) * 6,
        out_specs=(cells, cells, P(None, None, "gx", "gy")),
        check_vma=False,
    )
```

time: 24.2 us -> 21.2 us (0.88)
  waiting for transfers between devices: 8.55 us -> 4.42 us
  Pallas kernels: 5.18 us -> 6.63 us
  starting transfers between devices: 9.55 us -> 9.17 us
    ppermute x3, waiting for transfers between devices: 5.39 us -> 3.14 us  [shards(): blocks.append(lax.ppermute(sent[peer - 1] if packed else own, 'gy', ring))]
    ppermute x1, waiting for transfers between devices: 3.15 us -> 1.29 us  [shards(): outer = lax.ppermute(outer, 'gx', pairs[1])]
    pallas_call x3 -> x4, Pallas kernels: 5.18 us -> 6.63 us  [the longest x1 3.56 us: shards(): pl.pallas_call(functools.partial(last_kernel, count, rows_count, cols), o...]
    ppermute x1, starting transfers between devices: 2.87 us -> 1.6 us  [shards(): inner = lax.ppermute(inner, 'gx', pairs[0])]
    ppermute x3, starting transfers between devices: 3.58 us -> 4.47 us  [shards(): blocks.append(lax.ppermute(sent[peer - 1] if packed else own, 'gy', ring))]
  transfers between devices with their start and end apart: 5 -> 5, of which waited for: 4 -> 3; matrix products, arithmetic and copies ran while one was open for 0% -> 0% of each run, Pallas kernels for 0% -> 9%
where the time goes in v3:
time: 21.2 us; the launch traced here: 20.9 us
  starting transfers between devices  9.17 us (43%)
  Pallas kernels  6.63 us (31%)
  waiting for transfers between devices  4.42 us (21%)
  between operations  0.7 us (3%)
    ppermute x3, starting transfers between devices, shards(): blocks.append(lax.ppermute(sent[peer - 1] if packed else own, 'gy', ring))  4.47 us
    pallas_call x1, Pallas kernels, shards(): pl.pallas_call(functools.partial(last_kernel, count, rows_count, cols), o...  3.56 us
    ppermute x3, waiting for transfers between devices, shards(): blocks.append(lax.ppermute(sent[peer - 1] if packed else own, 'gy', ring))  3.14 us
    ppermute x1, starting transfers between devices, shards(): outer = lax.ppermute(outer, 'gx', pairs[1])  3.1 us
    pallas_call x1, Pallas kernels, shards(): pl.pallas_call(functools.partial(middle_kernel, count, packed), out_shape...  1.84 us
    ppermute x1, starting transfers between devices, shards(): inner = lax.ppermute(inner, 'gx', pairs[0])  1.6 us
    ppermute x1, waiting for transfers between devices, shards(): outer = lax.ppermute(outer, 'gx', pairs[1])  1.29 us
    pallas_call x1, Pallas kernels, shards(): pl.pallas_call(functools.partial(pack_kernel, count, packed), out_shape=(...  1.11 us
  transfers between devices with their start and end apart: 5, of which 3 were waited for; matrix products, arithmetic and copies ran while one was open for 0% of the time, Pallas kernels for 9%

profile of v3, /device:TPU:1, one launch (start us, length us, event | category | flops | bytes accessed | tf_op | source)
XLA Modules:
  0.0 20.9 jit_solution(13657753847927927924)
XLA Ops:
  0.6 1.1 %pack.1 = (f32[4,8,8,128]{3,2,1,0:T(8,128)S(1)}, f32[4,48,128]{2,1,0:T(8,128)S(1)}, f32[4,32,128]{2,1,0:T(8,128)S(1)}, f32[4,48,128]{2,1,0:T(8,128)S(1)}) custom-call(f32[8,8,128]{2,1,0:T(8,128)} %head_ref.1, f32[8,8,128]{2,1,0:T(8,128)} %temp_ref.1, s32[8,8,128]{2,1,0:T(8,128)} %soil_ref.1, s32[8,8,128]{2,1,0:T(8,128)} %ice_ref.1), custom_call_target="tpu_custom_call" | custom-call | tf_op jit(solution)/shard_map/pack/pallas_call | solution.py:394
  1.7 2.1 %collective-permute-start = (f32[4,48,128]{2,1,0:T(8,128)S(1)}, f32[4,48,128]{2,1,0:T(8,128)S(1)}, u32[]{:S(2)}, u32[]{:S(2)}) collective-permute-start(f32[4,48,128]{2,1,0:T(8,128)S(1)} %get-tuple-element.13), channel_id=1, source_target_pairs={{0,1},{1,2},{2,3},{3,0},{4,5},{5,6},{6,7},{7,4},{8,9},{9,10},{10,1... | collective-permute-start | bytes 294920 | tf_op jit(solution)/shard_map/ppermute | solution.py:409
  3.8 1.0 %collective-permute-start.2 = (f32[4,48,128]{2,1,0:T(8,128)S(1)}, f32[4,48,128]{2,1,0:T(8,128)S(1)}, u32[]{:S(2)}, u32[]{:S(2)}) collective-permute-start(f32[4,48,128]{2,1,0:T(8,128)S(1)} %get-tuple-element.15), channel_id=1, source_target_pairs={{0,3},{1,0},{2,1},{3,2},{4,7},{5,4},{6,5},{7,6},{8,11},{9,8},{10,9... | collective-permute-start | bytes 294920 | tf_op jit(solution)/shard_map/ppermute | solution.py:409
  4.8 1.4 %collective-permute-start.1 = (f32[4,32,128]{2,1,0:T(8,128)S(1)}, f32[4,32,128]{2,1,0:T(8,128)S(1)}, u32[]{:S(2)}, u32[]{:S(2)}) collective-permute-start(f32[4,32,128]{2,1,0:T(8,128)S(1)} %get-tuple-element.14), channel_id=1, source_target_pairs={{0,2},{1,3},{2,0},{3,1},{4,6},{5,7},{6,4},{7,5},{8,10},{9,11},{10,... | collective-permute-start | bytes 196616 | tf_op jit(solution)/shard_map/ppermute | solution.py:409
  6.2 2.6 %collective-permute-done.1.refs_2_ = f32[4,32,128]{2,1,0:T(8,128)S(1)} collective-permute-done((f32[4,32,128]{2,1,0:T(8,128)S(1)}, f32[4,32,128]{2,1,0:T(8,128)S(1)}, u32[]{:S(2)}, u32[]{:S(2)}) %collective-permute-start.1) | collective-permute-done | bytes 65568 | tf_op jit(solution)/shard_map/ppermute | solution.py:409
  8.8 0.0 collective-permute-done.refs_1_
  8.8 0.6 %collective-permute-done.2.refs_3_ = f32[4,48,128]{2,1,0:T(8,128)S(1)} collective-permute-done((f32[4,48,128]{2,1,0:T(8,128)S(1)}, f32[4,48,128]{2,1,0:T(8,128)S(1)}, u32[]{:S(2)}, u32[]{:S(2)}) %collective-permute-start.2) | collective-permute-done | bytes 98336 | tf_op jit(solution)/shard_map/ppermute | solution.py:409
  9.4 0.1 edges.1
  9.5 0.0 copy-start
  9.5 0.0 copy-start.1
  9.5 1.6 %collective-permute-start.3 = (f32[4,2,32,128]{3,2,1,0:T(8,128)S(1)}, f32[4,2,32,128]{3,2,1,0:T(8,128)S(1)}, u32[]{:S(2)}, u32[]{:S(2)}) collective-permute-start(f32[4,2,32,128]{3,2,1,0:T(8,128)S(1)} %get-tuple-element.16), channel_id=1, source_target_pairs={{0,4},{8,12},{16,20},{24,28},{4,0},{12,8},{20,16},{28,24},{1,5},{9... | collective-permute-start | bytes 393224 | tf_op jit(solution)/shard_map/ppermute | solution.py:424
  11.1 3.1 %collective-permute-start.4 = (f32[4,2,32,128]{3,2,1,0:T(8,128)S(1)}, f32[4,2,32,128]{3,2,1,0:T(8,128)S(1)}, u32[]{:S(2)}, u32[]{:S(2)}) collective-permute-start(f32[4,2,32,128]{3,2,1,0:T(8,128)S(1)} %get-tuple-element.17), channel_id=1, source_target_pairs={{4,8},{12,16},{20,24},{8,4},{16,12},{24,20},{5,9},{13,17},{21,25},... | collective-permute-start | bytes 393224 | tf_op jit(solution)/shard_map/ppermute | solution.py:423
  14.2 0.0 copy-done
  14.2 0.0 copy-done.1
  14.2 1.8 %within.1 = (f32[8,32,128]{2,1,0:T(8,128)S(1)}, f32[8,32,128]{2,1,0:T(8,128)S(1)}, f32[2,9,32,128]{3,2,1,0:T(8,128)S(1)}) custom-call(f32[12]{0:T(128)S(1)} %copy-done, f32[12]{0:T(128)S(1)} %copy-done.1, f32[4,8,8,128]{3,2,1,0:T(8,128)S(1)} %get-tuple-element.12.refs_0_, f32[4,48,128]{2,1,0:T(8,128)S(1)} %collective-permute-done.refs_1_, ...), custom_call_target="tpu_custom_call" | custom-call | tf_op jit(solution)/shard_map/within/pallas_call | solution.py:427
  16.1 0.0 collective-permute-done.3.inner_ref
  16.1 1.3 %collective-permute-done.4.outer_ref = f32[4,2,32,128]{3,2,1,0:T(8,128)S(1)} collective-permute-done((f32[4,2,32,128]{3,2,1,0:T(8,128)S(1)}, f32[4,2,32,128]{3,2,1,0:T(8,128)S(1)}, u32[]{:S(2)}, u32[]{:S(2)}) %collective-permute-start.4) | collective-permute-done | bytes 131104 | tf_op jit(solution)/shard_map/ppermute | solution.py:423
  17.4 3.6 %views.1 = (f32[8,8,128]{2,1,0:T(8,128)}, f32[8,8,128]{2,1,0:T(8,128)}, f32[4,4,8,32]{3,2,1,0:T(8,128)}) custom-call(f32[12]{0:T(128)S(1)} %copy-done, f32[12]{0:T(128)S(1)} %copy-done.1, f32[4]{0:T(128)} %tilt_from.1, f32[3]{0:T(128)} %gain_from.1, f32[3]{0:T(128)} %middle_from.1, s32[4,4]{1,0:T(4,128)} %rank_from.1, ...), custom_call_target="tpu_custom_call" | custom-call | tf_op jit(solution)/shard_map/views/pallas_call | solution.py:441
Async XLA Ops:
  1.7 7.0 %collective-permute-start = (f32[4,48,128]{2,1,0:T(8,128)S(1)}, f32[4,48,128]{2,1,0:T(8,128)S(1)}, u32[]{:S(2)}, u32[]{:S(2)}) collective-permute-start(f32[4,48,128]{2,1,0:T(8,128)S(1)} %get-tuple-element.13), channel_id=1, source_target_pairs={{0,1},{1,2},{2,3},{3,0},{4,5},{5,6},{6,7},{7,4},{8,9},{9,10},{10,1... | collective-permute-start | bytes 294920 | tf_op jit(solution)/shard_map/ppermute | solution.py:409
  3.8 5.5 %collective-permute-start.2 = (f32[4,48,128]{2,1,0:T(8,128)S(1)}, f32[4,48,128]{2,1,0:T(8,128)S(1)}, u32[]{:S(2)}, u32[]{:S(2)}) collective-permute-start(f32[4,48,128]{2,1,0:T(8,128)S(1)} %get-tuple-element.15), channel_id=1, source_target_pairs={{0,3},{1,0},{2,1},{3,2},{4,7},{5,4},{6,5},{7,6},{8,11},{9,8},{10,9... | collective-permute-start | bytes 294920 | tf_op jit(solution)/shard_map/ppermute | solution.py:409
  4.8 3.9 %collective-permute-start.1 = (f32[4,32,128]{2,1,0:T(8,128)S(1)}, f32[4,32,128]{2,1,0:T(8,128)S(1)}, u32[]{:S(2)}, u32[]{:S(2)}) collective-permute-start(f32[4,32,128]{2,1,0:T(8,128)S(1)} %get-tuple-element.14), channel_id=1, source_target_pairs={{0,2},{1,3},{2,0},{3,1},{4,6},{5,7},{6,4},{7,5},{8,10},{9,11},{10,... | collective-permute-start | bytes 196616 | tf_op jit(solution)/shard_map/ppermute | solution.py:409
  9.5 4.7 %copy-start = (f32[12]{0:T(128)S(1)}, f32[12]{0:T(128)}, u32[]{:S(2)}) copy-start(f32[12]{0:T(128)} %ks_ref.3) | copy-start | bytes 148
  9.5 4.7 %copy-start.1 = (f32[12]{0:T(128)S(1)}, f32[12]{0:T(128)}, u32[]{:S(2)}) copy-start(f32[12]{0:T(128)} %alpha_ref.3) | copy-start | bytes 148
  9.5 6.6 %collective-permute-start.3 = (f32[4,2,32,128]{3,2,1,0:T(8,128)S(1)}, f32[4,2,32,128]{3,2,1,0:T(8,128)S(1)}, u32[]{:S(2)}, u32[]{:S(2)}) collective-permute-start(f32[4,2,32,128]{3,2,1,0:T(8,128)S(1)} %get-tuple-element.16), channel_id=1, source_target_pairs={{0,4},{8,12},{16,20},{24,28},{4,0},{12,8},{20,16},{28,24},{1,5},{9... | collective-permute-start | bytes 393224 | tf_op jit(solution)/shard_map/ppermute | solution.py:424
  11.1 6.3 %collective-permute-start.4 = (f32[4,2,32,128]{3,2,1,0:T(8,128)S(1)}, f32[4,2,32,128]{3,2,1,0:T(8,128)S(1)}, u32[]{:S(2)}, u32[]{:S(2)}) collective-permute-start(f32[4,2,32,128]{3,2,1,0:T(8,128)S(1)} %get-tuple-element.17), channel_id=1, source_target_pairs={{4,8},{12,16},{20,24},{8,4},{16,12},{24,20},{5,9},{13,17},{21,25},... | collective-permute-start | bytes 393224 | tf_op jit(solution)/shard_map/ppermute | solution.py:423
